TPU v7x, 128 devices: a whole 4x4x4 slice. The times are simulated.
128 devices in a mesh: pb: 8 (over z, core), ka: 16 (over x, y).
Axes of the slice: x: 4, y: 4, z: 4, core: 2. Of those that a mesh axis runs over, the one named last changes fastest.
Arguments:
- queries: bfloat16 [16384, 2048], P('pb'), may hold values from -8 to 8
- keys: bfloat16 [16384, 2048], P(('ka', 'pb')), may hold values from -8 to 8
- values: bfloat16 [16384, 2048], P(('ka', 'pb')), may hold values from -6 to 6
- block_mask: int32 [128, 128], P('pb', 'ka'), may hold values from 0 to 1, as said below
Outputs:
- attended: bfloat16 [16384, 2048], P('pb')
Inputs may be any that keep to these rules, and one draw needn't show every extreme that they name: `block_mask`: 1 where the two blocks are equal or adjacent, in the first 2 block rows and block columns, and for 3 block columns drawn for each block row; 0 elsewhere.
All inputs are finite; a program needn't handle non-finite values.
Results may differ from a plain program's by a relative error of at most 0.0047.
Values may be sent and summed in bfloat16 or wider, within the bound.
A program may use at most 128 MiB of HBM per device.

v0:
```python
import jax
import jax.numpy as jnp
from jax import lax
from jax.sharding import PartitionSpec as P

HEADS = 16
HEAD_DIM = 128
BLOCK = 128


NEG = -1e30


def sent_to_all(shard, axis):
    length = lax.axis_size(axis)
    return lax.all_to_all(
        jnp.broadcast_to(shard[None], (length, *shard.shape)), axis, 0, 0, tiled=True
    )


def taken_together(shard, axis):
    everything = sent_to_all(shard, axis)
    return jnp.max(everything, axis=0)


def sent_together(arrays, axis, dim, along):
    ends, at = ([], 0)
    for a in arrays[:-1]:
        at += a.shape[along]
        ends.append(at)
    both = jnp.concatenate(arrays, axis=along)
    return tuple(
        jnp.split(lax.psum_scatter(both, axis, scatter_dimension=dim, tiled=True), ends, axis=along)
    )


def normalize_rows(numer, totals):
    row_count = numer.shape[0]
    shaped = numer.reshape(row_count, HEADS, HEAD_DIM) / totals[:, :, None]
    return shaped.reshape(row_count, HEADS * HEAD_DIM).astype(jnp.bfloat16)


def local(queries, keys, values, block_mask):
    key_panel, value_panel = (
        lax.all_gather(keys, "pb", axis=0, tiled=True),
        lax.all_gather(values, "pb", axis=0, tiled=True),
    )
    query_rows = queries.shape[0]
    allowed = jnp.repeat(jnp.repeat(block_mask > 0, BLOCK, axis=0), BLOCK, axis=1)
    scale = HEAD_DIM ** (-0.5)

    def head_scores(head_index):
        start = head_index * HEAD_DIM
        q_head = lax.dynamic_slice_in_dim(queries, start, HEAD_DIM, 1)
        k_head = lax.dynamic_slice_in_dim(key_panel, start, HEAD_DIM, 1)
        product = lax.dot_general(
            q_head, k_head, (((1,), (1,)), ((), ())), preferred_element_type=jnp.float32
        )
        return product * scale

    def local_top(scores):
        return jnp.max(jnp.where(allowed, scores, NEG), axis=1, keepdims=True)

    def accumulate(head_index, scores, head_top, numer, totals):
        weights = jnp.where(allowed, jnp.exp(scores - head_top), 0.0)
        totals = lax.dynamic_update_slice_in_dim(
            totals, jnp.sum(weights, axis=1, keepdims=True), head_index, 1
        )
        v_head = lax.dynamic_slice_in_dim(value_panel, head_index * HEAD_DIM, HEAD_DIM, 1)
        head_out = jnp.dot(weights.astype(jnp.bfloat16), v_head, preferred_element_type=jnp.float32)
        numer = lax.dynamic_update_slice_in_dim(numer, head_out, head_index * HEAD_DIM, 1)
        return (numer, totals)

    start_numer = jnp.zeros((query_rows, HEADS * HEAD_DIM), jnp.float32)
    start_totals = jnp.zeros((query_rows, HEADS), jnp.float32)

    def top_step(head_index, row_tops):
        largest = local_top(head_scores(head_index))
        return lax.dynamic_update_slice_in_dim(row_tops, largest, head_index, 1)

    row_tops = lax.fori_loop(0, HEADS, top_step, jnp.zeros((query_rows, HEADS), jnp.float32))
    row_tops = taken_together(row_tops, "ka")

    def value_step(head_index, carry):
        numer, totals = carry
        scores = head_scores(head_index)
        head_top = lax.dynamic_slice_in_dim(row_tops, head_index, 1, 1)
        return accumulate(head_index, scores, head_top, numer, totals)

    numer, totals = lax.fori_loop(0, HEADS, value_step, (start_numer, start_totals))
    numer, totals = sent_together((numer, totals), "ka", 0, 1)
    return lax.all_gather(normalize_rows(numer, totals), "ka", axis=0, tiled=True)


def solution(mesh):
    return jax.shard_map(
        local,
        mesh=mesh,
        in_specs=(P("pb", None), P(("ka", "pb"), None), P(("ka", "pb"), None), P("pb", "ka")),
        out_specs=P("pb", None),
        check_vma=False,
    )
```

profile of v0, /device:TPU:0, one launch (start us, length us, event | category | flops | bytes accessed | tf_op | source)
XLA Modules:
  0.0 507.8 jit_solution(3083225361864920179)
XLA Ops:
  6.5 0.7 all-gather.4.cloned.1.call-update
  7.3 0.7 all-gather.6.cloned.1.call-update
  8.0 0.7 broadcast_compare_fusion
  8.9 35.0 %all-gather.4.cloned.1.call-done = bf16[1024,2048]{1,0:T(8,128)(2,1)} async-done(((bf16[128,2048]{1,0:T(8,128)(2,1)}), bf16[1024,2048]{1,0:T(8,128)(2,1)}) %all-gather.4.cloned.1.call-update) | async-done | bytes 4194320 | tf_op jit(solution)/shard_map/all_gather | solution.py:45
  43.9 42.1 %while.30 = (s32[]{:T(128)}, f32[2048,16]{0,1:T(8,128)S(1)}, bf16[2048,2048]{1,0:T(8,128)(2,1)}, bf16[1024,2048]{1,0:T(8,128)(2,1)}, pred[2048,8]{0,1:T(8,128)(4...) while((s32[]{:T(128)}, f32[2048,16]{0,1:T(8,128)S(1)}, bf16[2048,2048]{1,0:T(8,128)(2,1)}, ...), condition=%wide.region_2.3_spmd.clone, body=%wide.region_0.2_spmd.clone.sunk | while | flops 543160320 | bytes 828567 | solution.py:81
  43.9 2.4 select_reduce_fusion.2
  46.5 2.4 select_reduce_fusion.2
  49.1 2.4 select_reduce_fusion.2
  51.7 2.4 select_reduce_fusion.2
  54.4 2.5 select_reduce_fusion.2
  57.1 2.4 select_reduce_fusion.2
  59.7 2.4 select_reduce_fusion.2
  62.3 2.4 select_reduce_fusion.2
  64.9 2.4 select_reduce_fusion.2
  67.6 2.4 select_reduce_fusion.2
  70.2 2.4 select_reduce_fusion.2
  72.8 2.4 select_reduce_fusion.2
  75.5 2.4 select_reduce_fusion.2
  78.1 2.4 select_reduce_fusion.2
  80.7 2.4 select_reduce_fusion.2
  83.3 2.4 select_reduce_fusion.2
  86.0 1.6 broadcast_in_dim.48
  87.5 6.8 %all-to-all-start = ((f32[16,2048,16]{1,2,0:T(8,128)}), f32[16,2048,16]{1,2,0:T(8,128)S(1)}, u32[]{:S(2)}, u32[]{:S(2)}) async-start(f32[16,2048,16]{1,2,0:T(8,128)} %broadcast_in_dim.48), calls=%async_computation | async-start | bytes 4194304 | tf_op jit(solution)/shard_map/all_to_all | solution.py:16
  94.4 30.7 %all-to-all-done = f32[16,2048,16]{1,2,0:T(8,128)S(1)} async-done(((f32[16,2048,16]{1,2,0:T(8,128)}), f32[16,2048,16]{1,2,0:T(8,128)S(1)}, u32[]{:S(2)}, u32[]{:S(2)}) %all-to-all-start) | async-done | bytes 2097184 | tf_op jit(solution)/shard_map/all_to_all | solution.py:16
  125.2 7.9 %broadcast_in_dim.45 = f32[2048,2048]{1,0:T(8,128)} broadcast(f32[]{:T(128)} %constant.104.clone.1), dimensions={} | broadcast | bytes 16777220 | tf_op jit(solution)/shard_map/broadcast_in_dim | solution.py:74
  133.1 159.8 %while.31 = (s32[]{:T(128)}, f32[2048,2048]{1,0:T(8,128)}, f32[2048,16]{0,1:T(8,128)S(1)}, bf16[2048,2048]{1,0:T(8,128)(2,1)}, bf16[1024,2048]{1,0:T(8,128)(2,1)...) while((s32[]{:T(128)}, f32[2048,2048]{1,0:T(8,128)}, ...), condition=%wide.region_6.7_spmd.clone, body=%wide.region_4.6_spmd.clone.sunk | while | flops 1084225536 | bytes 10553523 | solution.py:90
  133.1 5.3 %fusion.26 = (f32[2048]{0:T(1024)S(1)}, bf16[2048,1024]{0,1:T(8,128)(2,1)}) fusion(f32[2048]{0:T(1024)S(1)} %bitcast.33, pred[2048,8]{0,1:T(8,128)(4,1)S(1)} %get-tuple-element.444, bf16[1024,2048]{1,0:T(8,128)(2,1)} %get-tuple-element.441, s32[]{:T(128)S(6)} %select_n.61, bf16[2048,2048]{1,0:T(8,128)(2,1)} %get-tuple-element.440), kind=kOutput, calls=%fused_computation.7.clone.1 | convolution fusion | flops 547354624 | bytes 5014528 | tf_op jit(solution)/shard_map/while/body/eval_jaxpr/dot_general | solution.py:56
  138.6 4.5 convolution_dynamic-update-slice_fusion.2
  143.1 5.3 %fusion.26 = (f32[2048]{0:T(1024)S(1)}, bf16[2048,1024]{0,1:T(8,128)(2,1)}) fusion(f32[2048]{0:T(1024)S(1)} %bitcast.33, pred[2048,8]{0,1:T(8,128)(4,1)S(1)} %get-tuple-element.444, bf16[1024,2048]{1,0:T(8,128)(2,1)} %get-tuple-element.441, s32[]{:T(128)S(6)} %select_n.61, bf16[2048,2048]{1,0:T(8,128)(2,1)} %get-tuple-element.440), kind=kOutput, calls=%fused_computation.7.clone.1 | convolution fusion | flops 547354624 | bytes 5014528 | tf_op jit(solution)/shard_map/while/body/eval_jaxpr/dot_general | solution.py:56
  148.5 4.5 convolution_dynamic-update-slice_fusion.2
  153.1 5.3 %fusion.26 = (f32[2048]{0:T(1024)S(1)}, bf16[2048,1024]{0,1:T(8,128)(2,1)}) fusion(f32[2048]{0:T(1024)S(1)} %bitcast.33, pred[2048,8]{0,1:T(8,128)(4,1)S(1)} %get-tuple-element.444, bf16[1024,2048]{1,0:T(8,128)(2,1)} %get-tuple-element.441, s32[]{:T(128)S(6)} %select_n.61, bf16[2048,2048]{1,0:T(8,128)(2,1)} %get-tuple-element.440), kind=kOutput, calls=%fused_computation.7.clone.1 | convolution fusion | flops 547354624 | bytes 5014528 | tf_op jit(solution)/shard_map/while/body/eval_jaxpr/dot_general | solution.py:56
  158.5 4.5 convolution_dynamic-update-slice_fusion.2
  163.0 5.3 %fusion.26 = (f32[2048]{0:T(1024)S(1)}, bf16[2048,1024]{0,1:T(8,128)(2,1)}) fusion(f32[2048]{0:T(1024)S(1)} %bitcast.33, pred[2048,8]{0,1:T(8,128)(4,1)S(1)} %get-tuple-element.444, bf16[1024,2048]{1,0:T(8,128)(2,1)} %get-tuple-element.441, s32[]{:T(128)S(6)} %select_n.61, bf16[2048,2048]{1,0:T(8,128)(2,1)} %get-tuple-element.440), kind=kOutput, calls=%fused_computation.7.clone.1 | convolution fusion | flops 547354624 | bytes 5014528 | tf_op jit(solution)/shard_map/while/body/eval_jaxpr/dot_general | solution.py:56
  168.5 4.5 convolution_dynamic-update-slice_fusion.2
  173.0 5.3 %fusion.26 = (f32[2048]{0:T(1024)S(1)}, bf16[2048,1024]{0,1:T(8,128)(2,1)}) fusion(f32[2048]{0:T(1024)S(1)} %bitcast.33, pred[2048,8]{0,1:T(8,128)(4,1)S(1)} %get-tuple-element.444, bf16[1024,2048]{1,0:T(8,128)(2,1)} %get-tuple-element.441, s32[]{:T(128)S(6)} %select_n.61, bf16[2048,2048]{1,0:T(8,128)(2,1)} %get-tuple-element.440), kind=kOutput, calls=%fused_computation.7.clone.1 | convolution fusion | flops 547354624 | bytes 5014528 | tf_op jit(solution)/shard_map/while/body/eval_jaxpr/dot_general | solution.py:56
  178.5 4.5 convolution_dynamic-update-slice_fusion.2
  183.0 5.3 %fusion.26 = (f32[2048]{0:T(1024)S(1)}, bf16[2048,1024]{0,1:T(8,128)(2,1)}) fusion(f32[2048]{0:T(1024)S(1)} %bitcast.33, pred[2048,8]{0,1:T(8,128)(4,1)S(1)} %get-tuple-element.444, bf16[1024,2048]{1,0:T(8,128)(2,1)} %get-tuple-element.441, s32[]{:T(128)S(6)} %select_n.61, bf16[2048,2048]{1,0:T(8,128)(2,1)} %get-tuple-element.440), kind=kOutput, calls=%fused_computation.7.clone.1 | convolution fusion | flops 547354624 | bytes 5014528 | tf_op jit(solution)/shard_map/while/body/eval_jaxpr/dot_general | solution.py:56
  188.4 4.5 convolution_dynamic-update-slice_fusion.2
  193.0 5.3 %fusion.26 = (f32[2048]{0:T(1024)S(1)}, bf16[2048,1024]{0,1:T(8,128)(2,1)}) fusion(f32[2048]{0:T(1024)S(1)} %bitcast.33, pred[2048,8]{0,1:T(8,128)(4,1)S(1)} %get-tuple-element.444, bf16[1024,2048]{1,0:T(8,128)(2,1)} %get-tuple-element.441, s32[]{:T(128)S(6)} %select_n.61, bf16[2048,2048]{1,0:T(8,128)(2,1)} %get-tuple-element.440), kind=kOutput, calls=%fused_computation.7.clone.1 | convolution fusion | flops 547354624 | bytes 5014528 | tf_op jit(solution)/shard_map/while/body/eval_jaxpr/dot_general | solution.py:56
  198.4 4.5 convolution_dynamic-update-slice_fusion.2
  202.9 5.3 %fusion.26 = (f32[2048]{0:T(1024)S(1)}, bf16[2048,1024]{0,1:T(8,128)(2,1)}) fusion(f32[2048]{0:T(1024)S(1)} %bitcast.33, pred[2048,8]{0,1:T(8,128)(4,1)S(1)} %get-tuple-element.444, bf16[1024,2048]{1,0:T(8,128)(2,1)} %get-tuple-element.441, s32[]{:T(128)S(6)} %select_n.61, bf16[2048,2048]{1,0:T(8,128)(2,1)} %get-tuple-element.440), kind=kOutput, calls=%fused_computation.7.clone.1 | convolution fusion | flops 547354624 | bytes 5014528 | tf_op jit(solution)/shard_map/while/body/eval_jaxpr/dot_general | solution.py:56
  208.4 4.6 convolution_dynamic-update-slice_fusion.2
  213.0 5.3 %fusion.26 = (f32[2048]{0:T(1024)S(1)}, bf16[2048,1024]{0,1:T(8,128)(2,1)}) fusion(f32[2048]{0:T(1024)S(1)} %bitcast.33, pred[2048,8]{0,1:T(8,128)(4,1)S(1)} %get-tuple-element.444, bf16[1024,2048]{1,0:T(8,128)(2,1)} %get-tuple-element.441, s32[]{:T(128)S(6)} %select_n.61, bf16[2048,2048]{1,0:T(8,128)(2,1)} %get-tuple-element.440), kind=kOutput, calls=%fused_computation.7.clone.1 | convolution fusion | flops 547354624 | bytes 5014528 | tf_op jit(solution)/shard_map/while/body/eval_jaxpr/dot_general | solution.py:56
  218.4 4.5 convolution_dynamic-update-slice_fusion.2
  222.9 5.3 %fusion.26 = (f32[2048]{0:T(1024)S(1)}, bf16[2048,1024]{0,1:T(8,128)(2,1)}) fusion(f32[2048]{0:T(1024)S(1)} %bitcast.33, pred[2048,8]{0,1:T(8,128)(4,1)S(1)} %get-tuple-element.444, bf16[1024,2048]{1,0:T(8,128)(2,1)} %get-tuple-element.441, s32[]{:T(128)S(6)} %select_n.61, bf16[2048,2048]{1,0:T(8,128)(2,1)} %get-tuple-element.440), kind=kOutput, calls=%fused_computation.7.clone.1 | convolution fusion | flops 547354624 | bytes 5014528 | tf_op jit(solution)/shard_map/while/body/eval_jaxpr/dot_general | solution.py:56
  228.4 4.6 convolution_dynamic-update-slice_fusion.2
  232.9 5.3 %fusion.26 = (f32[2048]{0:T(1024)S(1)}, bf16[2048,1024]{0,1:T(8,128)(2,1)}) fusion(f32[2048]{0:T(1024)S(1)} %bitcast.33, pred[2048,8]{0,1:T(8,128)(4,1)S(1)} %get-tuple-element.444, bf16[1024,2048]{1,0:T(8,128)(2,1)} %get-tuple-element.441, s32[]{:T(128)S(6)} %select_n.61, bf16[2048,2048]{1,0:T(8,128)(2,1)} %get-tuple-element.440), kind=kOutput, calls=%fused_computation.7.clone.1 | convolution fusion | flops 547354624 | bytes 5014528 | tf_op jit(solution)/shard_map/while/body/eval_jaxpr/dot_general | solution.py:56
  238.4 4.6 convolution_dynamic-update-slice_fusion.2
  243.0 5.3 %fusion.26 = (f32[2048]{0:T(1024)S(1)}, bf16[2048,1024]{0,1:T(8,128)(2,1)}) fusion(f32[2048]{0:T(1024)S(1)} %bitcast.33, pred[2048,8]{0,1:T(8,128)(4,1)S(1)} %get-tuple-element.444, bf16[1024,2048]{1,0:T(8,128)(2,1)} %get-tuple-element.441, s32[]{:T(128)S(6)} %select_n.61, bf16[2048,2048]{1,0:T(8,128)(2,1)} %get-tuple-element.440), kind=kOutput, calls=%fused_computation.7.clone.1 | convolution fusion | flops 547354624 | bytes 5014528 | tf_op jit(solution)/shard_map/while/body/eval_jaxpr/dot_general | solution.py:56
  248.4 4.5 convolution_dynamic-update-slice_fusion.2
  252.9 5.3 %fusion.26 = (f32[2048]{0:T(1024)S(1)}, bf16[2048,1024]{0,1:T(8,128)(2,1)}) fusion(f32[2048]{0:T(1024)S(1)} %bitcast.33, pred[2048,8]{0,1:T(8,128)(4,1)S(1)} %get-tuple-element.444, bf16[1024,2048]{1,0:T(8,128)(2,1)} %get-tuple-element.441, s32[]{:T(128)S(6)} %select_n.61, bf16[2048,2048]{1,0:T(8,128)(2,1)} %get-tuple-element.440), kind=kOutput, calls=%fused_computation.7.clone.1 | convolution fusion | flops 547354624 | bytes 5014528 | tf_op jit(solution)/shard_map/while/body/eval_jaxpr/dot_general | solution.py:56
  258.4 4.6 convolution_dynamic-update-slice_fusion.2
  263.0 5.3 %fusion.26 = (f32[2048]{0:T(1024)S(1)}, bf16[2048,1024]{0,1:T(8,128)(2,1)}) fusion(f32[2048]{0:T(1024)S(1)} %bitcast.33, pred[2048,8]{0,1:T(8,128)(4,1)S(1)} %get-tuple-element.444, bf16[1024,2048]{1,0:T(8,128)(2,1)} %get-tuple-element.441, s32[]{:T(128)S(6)} %select_n.61, bf16[2048,2048]{1,0:T(8,128)(2,1)} %get-tuple-element.440), kind=kOutput, calls=%fused_computation.7.clone.1 | convolution fusion | flops 547354624 | bytes 5014528 | tf_op jit(solution)/shard_map/while/body/eval_jaxpr/dot_general | solution.py:56
  268.4 4.5 convolution_dynamic-update-slice_fusion.2
  272.9 5.3 %fusion.26 = (f32[2048]{0:T(1024)S(1)}, bf16[2048,1024]{0,1:T(8,128)(2,1)}) fusion(f32[2048]{0:T(1024)S(1)} %bitcast.33, pred[2048,8]{0,1:T(8,128)(4,1)S(1)} %get-tuple-element.444, bf16[1024,2048]{1,0:T(8,128)(2,1)} %get-tuple-element.441, s32[]{:T(128)S(6)} %select_n.61, bf16[2048,2048]{1,0:T(8,128)(2,1)} %get-tuple-element.440), kind=kOutput, calls=%fused_computation.7.clone.1 | convolution fusion | flops 547354624 | bytes 5014528 | tf_op jit(solution)/shard_map/while/body/eval_jaxpr/dot_general | solution.py:56
  278.4 4.5 convolution_dynamic-update-slice_fusion.2
  282.9 5.3 %fusion.26 = (f32[2048]{0:T(1024)S(1)}, bf16[2048,1024]{0,1:T(8,128)(2,1)}) fusion(f32[2048]{0:T(1024)S(1)} %bitcast.33, pred[2048,8]{0,1:T(8,128)(4,1)S(1)} %get-tuple-element.444, bf16[1024,2048]{1,0:T(8,128)(2,1)} %get-tuple-element.441, s32[]{:T(128)S(6)} %select_n.61, bf16[2048,2048]{1,0:T(8,128)(2,1)} %get-tuple-element.440), kind=kOutput, calls=%fused_computation.7.clone.1 | convolution fusion | flops 547354624 | bytes 5014528 | tf_op jit(solution)/shard_map/while/body/eval_jaxpr/dot_general | solution.py:56
  288.3 4.6 convolution_dynamic-update-slice_fusion.2
  293.2 11.6 %pad_maximum_fusion = f32[2048,2064]{1,0:T(8,128)} fusion(f32[2048,16]{1,0:T(8,128)S(1)} %copy.9, f32[2048,2048]{1,0:T(8,128)} %get-tuple-element.240), kind=kLoop, calls=%fused_computation.17 | loop fusion | flops 4227072 | bytes 33816576 | tf_op jit(solution)/shard_map/concatenate | solution.py:31
  304.9 114.0 %reduce-scatter.2.cloned.1.call-done = f32[128,2064]{1,0:T(8,128)} async-done(((f32[2048,2064]{1,0:T(8,128)}), f32[128,2064]{1,0:T(8,128)}) %reduce-scatter.2.cloned.1.call-update) | async-done | bytes 1056784 | tf_op jit(solution)/shard_map/reduce_scatter | solution.py:33
  418.9 0.8 split.9
  420.1 2.4 fusion.15
  422.5 70.4 %all-gather.8.cloned.1.call-done = bf16[2048,2048]{1,0:T(8,128)(2,1)} async-done(((bf16[128,2048]{1,0:T(8,128)(2,1)}), bf16[2048,2048]{1,0:T(8,128)(2,1)}) %all-gather.8.cloned.1.call-update) | async-done | bytes 8388624 | tf_op jit(solution)/shard_map/all_gather | solution.py:92
  492.9 8.4 %copy.31 = bf16[2048,2048]{1,0:T(8,128)(2,1)} copy(bf16[2048,2048]{1,0:T(8,128)(2,1)} %all-gather.8.cloned.1.call-done) | data formatting | bytes 16777216
  (62 shorter events, 7.2 us)
Async XLA Ops:
  6.5 37.3 %all-gather.4.cloned.1.call-start = ((), (), s32[]{:S(2)}) async-start(), calls=%async_computation.2 | async-start | bytes 4718592 | tf_op jit(solution)/shard_map/all_gather | solution.py:45
  7.3 118.0 %all-gather.6.cloned.1.call-start = ((), (), s32[]{:S(2)}) async-start(), calls=%async_computation.3 | async-start | bytes 4718592 | tf_op jit(solution)/shard_map/all_gather | solution.py:46
  87.5 37.6 %all-to-all-start = ((f32[16,2048,16]{1,2,0:T(8,128)}), f32[16,2048,16]{1,2,0:T(8,128)S(1)}, u32[]{:S(2)}, u32[]{:S(2)}) async-start(f32[16,2048,16]{1,2,0:T(8,128)} %broadcast_in_dim.48), calls=%async_computation | async-start | bytes 4194304 | tf_op jit(solution)/shard_map/all_to_all | solution.py:16
  94.3 324.6 %reduce-scatter.2.cloned.1.call-start = ((), (), s32[]{:S(2)}) async-start(), calls=%async_computation.4 | async-start | bytes 18939904 | tf_op jit(solution)/shard_map/reduce_scatter | solution.py:33
  304.9 188.0 %all-gather.8.cloned.1.call-start = ((), (), s32[]{:S(2)}) async-start(), calls=%async_computation.5 | async-start | bytes 8912896 | tf_op jit(solution)/shard_map/all_gather | solution.py:92
Sparse Core Ops, SparseCore 0:
  9.0 34.7 all-gather.3
  45.6 32.0 all-gather.5
  305.0 113.8 reduce-scatter.1
  422.6 70.1 all-gather.7
where the time goes:
time: 509 us; the launch traced here: 508 us
  waiting for transfers between devices  251 us (49%)
  matrix products  195 us (38%)
  local copies, waits for them, and re-layouts  25.6 us (5%)
  other arithmetic  14.8 us (3%)
  between operations  13.2 us (3%)
  starting transfers between devices  6.94 us (1%)
    dot_general x32, matrix products, head_scores(): lax.dot_general(q_head, k_head, (((1,), (1,)), ((), ())), preferred_eleme...  123 us
    reduce_scatter x1, waiting for transfers between devices, sent_together(): lax.psum_scatter(both, axis, scatter_dimension=dim, tiled=True)  114 us
    dot_general x16, matrix products, accumulate(): jnp.dot(weights.astype(jnp.bfloat16), v_head, preferred_element_type=jnp....  72.5 us
    all_gather x1, waiting for transfers between devices, local(): lax.all_gather(normalize_rows(numer, totals), 'ka', axis=0, tiled=True)  70.4 us
    all_gather x1, waiting for transfers between devices, local(): lax.all_gather(keys, 'pb', axis=0, tiled=True)  35 us
    all_to_all x1, waiting for transfers between devices, sent_to_all(): lax.all_to_all(jnp.broadcast_to(shard[None], (length, *shard.shape)), axi...  30.7 us
    concatenate x1, other arithmetic, sent_together(): both = jnp.concatenate(arrays, axis=along)  11.6 us
  transfers between devices with their start and end apart: 5, of which 4 were waited for; matrix products, arithmetic and copies ran while one was open for 9% of the time, Pallas kernels for 0%

commit v1 on v0

v1 whole, which is shorter than its diff:
```python
import functools

import jax
import jax.numpy as jnp
from jax import lax
from jax.experimental import pallas as pl
from jax.experimental.pallas import tpu as pltpu
from jax.sharding import PartitionSpec as P

HEADS = 16
HEAD_DIM = 128
BLOCK = 128
NPB = 8
NKA = 16
ROWS = 2048
QBLOCKS = ROWS // BLOCK
SLOTS = 8
MESH = pl.DeviceIdType.MESH
BF16 = jnp.bfloat16
F32 = jnp.float32
SCALE = HEAD_DIM ** (-0.5) * 1.4426950408889634
NEG = -1e30


def remote(src, dst, send, recv, pb, ka):
    return pltpu.make_async_remote_copy(
        src_ref=src,
        dst_ref=dst,
        send_sem=send,
        recv_sem=recv,
        device_id={"pb": pb, "ka": ka},
        device_id_type=MESH,
    )


def greet(peers):
    barrier = pltpu.get_barrier_semaphore()
    for pb, ka in peers:
        pl.semaphore_signal(
            barrier, inc=1, device_id={"pb": pb, "ka": ka}, device_id_type=MESH
        )
    pl.semaphore_wait(barrier, len(peers))


def gather_kernel(
    k_ref, v_ref, m_ref, kb_ref, vb_ref, mb_ref,
    own_sem, a_send, a_recv, m_send, m_recv, z_send, z_recv,
):
    pb = lax.axis_index("pb")
    ka = lax.axis_index("ka")
    other = pb + 1 - 2 * (pb % 2)
    up = (pb + 2) % NPB
    down = (pb + 6) % NPB
    far = (pb + 4) % NPB

    def peer_of(d):
        hi, lo = ka // 4, ka % 4

        def xor2(a, b):
            if b == 0:
                return a
            if b == 1:
                return a + 1 - 2 * (a % 2)
            if b == 2:
                return (a + 2) % 4
            return 3 - a

        return xor2(hi, d // 4) * 4 + xor2(lo, d % 4)

    peers = [peer_of(d) for d in range(NKA)]
    greet(
        [(pb, peers[d]) for d in range(1, NKA)] + [(other, ka), (up, ka), (down, ka)]
    )

    def cols(i):
        return pl.ds(pl.multiple_of(i * HEAD_DIM, HEAD_DIM), HEAD_DIM)

    srcs, bufs = (k_ref, v_ref), (kb_ref, vb_ref)
    owns = []
    for t in range(2):
        c = pltpu.make_async_copy(srcs[t].at[:, cols(ka)], bufs[t].at[pb, ka], own_sem.at[t])
        c.start()
        owns.append(c)
    own_m = pltpu.make_async_copy(m_ref, mb_ref.at[ka], own_sem.at[2])
    own_m.start()
    sends = []
    for t in range(2):
        for d in range(1, NKA):
            c = remote(
                srcs[t].at[:, cols(peers[d])], bufs[t].at[pb, ka],
                a_send.at[t, d], a_recv.at[t, d], pb, peers[d],
            )
            c.start()
            sends.append(c)
    for d in range(1, NKA):
        c = remote(m_ref, mb_ref.at[ka], m_send.at[d], m_recv.at[d], pb, peers[d])
        c.start()
        sends.append(c)

    def group(buf, who, g, first=0, count=4):
        base = (peers[4 * g] // 4) * 4 + first
        return buf.at[who, pl.ds(base, count)]

    def send(kind, step, ref, to):
        c = remote(ref, ref, z_send.at[kind, step], z_recv.at[kind, step], to, ka)
        c.start()
        sends.append(c)

    def arrived(kind, step, ref):
        remote(ref, ref, z_send.at[kind, step], z_recv.at[kind, step], up, ka).wait_recv()

    for step in range(10):
        if step < 8:
            t, g = divmod(step, 4)
            if g == 0:
                owns[t].wait()
            for d in range(4 * g, 4 * g + 4):
                if d:
                    ref = bufs[t].at[pb, peers[d]]
                    remote(ref, ref, a_send.at[t, d], a_recv.at[t, d], pb, ka).wait_recv()
            mine = group(bufs[t], pb, g)
            send(0, step, mine, up)
            send(1, step, mine, down)
            send(2, step, mine, other)
        if 1 <= step < 9:
            t, g = divmod(step - 1, 4)
            low = group(bufs[t], down, g)
            arrived(0, step - 1, low)
            send(3, step - 1, group(bufs[t], down, g, 0, 2), up)
            send(5, step - 1, low, other)
            high = group(bufs[t], up, g)
            arrived(1, step - 1, high)
            send(4, step - 1, group(bufs[t], up, g, 2, 2), down)
            send(6, step - 1, high, other)
        if 2 <= step:
            t, g = divmod(step - 2, 4)
            a = group(bufs[t], far, g, 0, 2)
            arrived(3, step - 2, a)
            send(7, step - 2, a, other)
            b = group(bufs[t], far, g, 2, 2)
            arrived(4, step - 2, b)
            send(8, step - 2, b, other)
    ob = other
    for step in range(8):
        t, g = divmod(step, 4)
        arrived(2, step, group(bufs[t], ob, g))
        arrived(5, step, group(bufs[t], (ob + 6) % NPB, g))
        arrived(6, step, group(bufs[t], (ob + 2) % NPB, g))
        arrived(7, step, group(bufs[t], (ob + 4) % NPB, g, 0, 2))
        arrived(8, step, group(bufs[t], (ob + 4) % NPB, g, 2, 2))
    own_m.wait()
    for d in range(1, NKA):
        ref = mb_ref.at[peers[d]]
        remote(ref, ref, m_send.at[d], m_recv.at[d], pb, ka).wait_recv()
    for c in sends:
        c.wait_send()


def gather(keys, values, mask_t):
    shape = jax.ShapeDtypeStruct((NPB, NKA, BLOCK, HEAD_DIM), BF16)
    any_spec = pl.BlockSpec(memory_space=pl.ANY)
    dma = pltpu.SemaphoreType.DMA
    return pl.pallas_call(
        gather_kernel,
        out_shape=(shape, shape, jax.ShapeDtypeStruct((NKA, 8, 128), jnp.int32)),
        in_specs=[any_spec] * 3,
        out_specs=(any_spec,) * 3,
        scratch_shapes=[
            dma((3,)), dma((2, NKA)), dma((2, NKA)), dma((NKA,)), dma((NKA,)),
            dma((9, 8)), dma((9, 8)),
        ],
        compiler_params=pltpu.CompilerParams(collective_id=0, has_side_effects=True),
        name="gather",
    )(keys, values, mask_t)


def attend_kernel(
    q_hbm, k_hbm, v_hbm, m_ref, o_hbm,
    q_ref, k_ref, v_ref, o_ref, tab_v, tab_s, acc, top, tot, sems,
):
    pb = lax.axis_index("pb")
    ka = lax.axis_index("ka")
    qc = pltpu.make_async_copy(
        q_hbm.at[:, pl.ds(pl.multiple_of(ka * HEAD_DIM, HEAD_DIM), HEAD_DIM)], q_ref, sems.at[0]
    )
    kc = pltpu.make_async_copy(k_hbm, k_ref, sems.at[1])
    vc = pltpu.make_async_copy(v_hbm, v_ref, sems.at[2])
    qc.start()
    kc.start()
    vc.start()

    live = (m_ref[...].reshape(NKA * 8, 128) > 0).astype(F32)
    row = lax.broadcasted_iota(jnp.int32, (128, 128), 0)
    col = lax.broadcasted_iota(jnp.int32, (128, 128), 1)
    lower = (col <= row).astype(F32)
    rank = jnp.dot(lower.astype(BF16), live.astype(BF16), preferred_element_type=F32)
    weight = live * row.astype(F32)
    parts = [
        jnp.sum(jnp.where(rank == s + 1, weight, 0.0), axis=0, keepdims=True)
        for s in range(SLOTS)
    ]
    count = jnp.sum(live, axis=0, keepdims=True)
    table = jnp.concatenate(parts + [jnp.broadcast_to(count, (8, 128))], axis=0)
    tab_v[...] = table.astype(jnp.int32)
    tc = pltpu.make_async_copy(tab_v, tab_s, sems.at[3])
    tc.start()
    tc.wait()
    qc.wait()
    kc.wait()
    vc.wait()

    first = jnp.where(pb == 0, 2, 0)

    def scores(q, k):
        return lax.dot_general(q, k, (((1,), (1,)), ((), ())), preferred_element_type=F32)

    def block(i, carry):
        rows = pl.ds(pl.multiple_of(i * BLOCK, BLOCK), BLOCK)
        q = q_ref[rows, :]
        n = tab_s[SLOTS, i]
        js = [tab_s[s, i] for s in range(SLOTS)]
        ss = []
        for s in range(SLOTS):
            k = k_ref[js[s] % NPB, js[s] // NPB]
            ss.append(scores(q, k) * SCALE + jnp.where(s < n, 0.0, NEG))
        m = ss[0]
        for s in range(1, SLOTS):
            m = jnp.maximum(m, ss[s])
        m = jnp.max(m, axis=1, keepdims=True)
        total = None
        out = None
        for s in range(SLOTS):
            p = jnp.exp2(ss[s] - m)
            total = p if total is None else total + p
            v = v_ref[js[s] % NPB, js[s] // NPB]
            o = jnp.dot(p.astype(BF16), v, preferred_element_type=F32)
            out = o if out is None else out + o
        out = out / jnp.sum(total, axis=1, keepdims=True)
        o_ref[rows, :] = out.astype(BF16)
        return carry

    lax.fori_loop(first, QBLOCKS, block, 0)

    @pl.when(pb == 0)
    def _():
        q = q_ref[0 : 2 * BLOCK, :]
        acc[...] = jnp.zeros_like(acc)
        tot[...] = jnp.zeros_like(tot)
        top[...] = jnp.full_like(top, NEG)

        def chunk(c, carry):
            b, half = c // 2, c % 2
            k = k_ref[b, pl.ds(half * 8, 8)].reshape(8 * BLOCK, HEAD_DIM)
            v = v_ref[b, pl.ds(half * 8, 8)].reshape(8 * BLOCK, HEAD_DIM)
            s = scores(q, k) * SCALE
            old = top[...]
            m = jnp.maximum(old, jnp.max(s, axis=1, keepdims=True))
            p = jnp.exp2(s - m[:, :1])
            a = jnp.exp2(old - m)
            tot[...] = a * tot[...] + jnp.sum(p, axis=1, keepdims=True)
            acc[...] = a * acc[...] + jnp.dot(p.astype(BF16), v, preferred_element_type=F32)
            top[...] = m
            return carry

        lax.fori_loop(0, 16, chunk, 0)
        o_ref[0 : 2 * BLOCK, :] = (acc[...] / tot[...]).astype(BF16)

    oc = pltpu.make_async_copy(o_ref, o_hbm.at[ka], sems.at[4])
    oc.start()
    oc.wait()


def attend(queries, kbuf, vbuf, mbuf):
    any_spec = pl.BlockSpec(memory_space=pl.ANY)
    shape = (NPB, NKA, BLOCK, HEAD_DIM)
    return pl.pallas_call(
        attend_kernel,
        out_shape=jax.ShapeDtypeStruct((NKA, ROWS, HEAD_DIM), BF16),
        in_specs=[any_spec] * 3 + [pl.BlockSpec(memory_space=pltpu.VMEM)],
        out_specs=any_spec,
        scratch_shapes=[
            pltpu.VMEM((ROWS, HEAD_DIM), BF16),
            pltpu.VMEM(shape, BF16),
            pltpu.VMEM(shape, BF16),
            pltpu.VMEM((ROWS, HEAD_DIM), BF16),
            pltpu.VMEM((16, 128), jnp.int32),
            pltpu.SMEM((16, 128), jnp.int32),
            pltpu.VMEM((2 * BLOCK, HEAD_DIM), F32),
            pltpu.VMEM((2 * BLOCK, HEAD_DIM), F32),
            pltpu.VMEM((2 * BLOCK, HEAD_DIM), F32),
            pltpu.SemaphoreType.DMA((5,)),
        ],
        name="attend",
    )(queries, kbuf, vbuf, mbuf)


HALF = ROWS // 2
PIECE = ROWS // 4


def spread_kernel(in_ref, out_ref, send_sem, recv_sem):
    del in_ref
    pb = lax.axis_index("pb")
    ka = lax.axis_index("ka")
    x, y = ka // 4, ka % 4

    def at(dx, dy):
        return ((x + dx + 4) % 4) * 4 + (y + dy + 4) % 4

    greet([(pb, at(1, 0)), (pb, at(3, 0)), (pb, at(0, 1)), (pb, at(0, 3))])
    sends = []

    def place(a, u, w):
        return at(u, w) if a == 0 else at(w, u)

    def ref(a, u, w, piece):
        lo, n = (0, 2) if piece is None else (piece, 1)
        return out_ref.at[place(a, u, w), pl.ds(a * HALF + lo * PIECE, n * PIECE)]

    def sem_id(u, w, piece):
        return ((u % 4) * 4 + w % 4) * 3 + (2 if piece is None else piece)

    def send(a, u, w, piece, du, dw):
        i = sem_id(u - du, w - dw, piece)
        r = ref(a, u, w, piece)
        c = remote(r, r, send_sem.at[a, i], recv_sem.at[a, i], pb, place(a, du, dw))
        c.start()
        sends.append(c)

    def arrived(a, u, w, piece):
        i = sem_id(u, w, piece)
        r = ref(a, u, w, piece)
        remote(r, r, send_sem.at[a, i], recv_sem.at[a, i], pb, ka).wait_recv()

    both = (0, 1)
    for a in both:
        send(a, 0, 0, None, 1, 0)
        send(a, 0, 0, None, -1, 0)
    for a in both:
        send(a, 0, 0, None, 0, 1)
        send(a, 0, 0, None, 0, -1)
    for a in both:
        arrived(a, -1, 0, None)
        send(a, -1, 0, 0, 1, 0)
        arrived(a, 1, 0, None)
        send(a, 1, 0, 1, -1, 0)
    for a in both:
        for u in (-1, 1):
            send(a, u, 0, None, 0, 1)
            send(a, u, 0, None, 0, -1)
    for a in both:
        arrived(a, 0, -1, None)
        send(a, 0, -1, 0, 0, 1)
        arrived(a, 0, 1, None)
        send(a, 0, 1, 1, 0, -1)
    for a in both:
        for piece in (0, 1):
            arrived(a, 2, 0, piece)
            send(a, 2, 0, piece, 0, 1)
            send(a, 2, 0, piece, 0, -1)
    for u in (-1, 1):
        for a in both:
            arrived(a, u, -1, None)
            send(a, u, -1, 0, 0, 1)
            arrived(a, u, 1, None)
            send(a, u, 1, 1, 0, -1)
    for a in both:
        arrived(a, 2, -1, 0)
        send(a, 2, -1, 0, 0, 1)
        arrived(a, 2, 1, 0)
    for a in both:
        arrived(a, 2, 1, 1)
        send(a, 2, 1, 1, 0, -1)
        arrived(a, 2, -1, 1)
    for a in both:
        for u in (0, -1, 1, 2):
            for piece in (0, 1):
                arrived(a, u, 2, piece)
    for c in sends:
        c.wait_send()


def spread(mine):
    any_spec = pl.BlockSpec(memory_space=pl.ANY)
    return pl.pallas_call(
        spread_kernel,
        out_shape=jax.ShapeDtypeStruct((NKA, ROWS, HEAD_DIM), BF16),
        in_specs=[any_spec],
        out_specs=any_spec,
        input_output_aliases={0: 0},
        scratch_shapes=[pltpu.SemaphoreType.DMA((2, 48)), pltpu.SemaphoreType.DMA((2, 48))],
        compiler_params=pltpu.CompilerParams(collective_id=1, has_side_effects=True),
        name="spread",
    )(mine)


def weave_kernel(in_ref, out_ref):
    out_ref[...] = in_ref[0]


def weave(heads):
    return pl.pallas_call(
        weave_kernel,
        out_shape=jax.ShapeDtypeStruct((ROWS, HEADS * HEAD_DIM), BF16),
        grid=(HEADS,),
        in_specs=[pl.BlockSpec((1, ROWS, HEAD_DIM), lambda h: (h, 0, 0))],
        out_specs=pl.BlockSpec((ROWS, HEAD_DIM), lambda h: (0, h)),
        name="weave",
    )(heads)


def local(queries, keys, values, block_mask):
    mask_t = jnp.pad(block_mask.T, ((0, 0), (0, 112)))
    kbuf, vbuf, mbuf = gather(keys, values, mask_t)
    mine = attend(queries, kbuf, vbuf, mbuf)
    return weave(spread(mine))


def solution(mesh):
    return jax.shard_map(
        local,
        mesh=mesh,
        in_specs=(P("pb", None), P(("ka", "pb"), None), P(("ka", "pb"), None), P("pb", "ka")),
        out_specs=P("pb", None),
        check_vma=False,
    )
```

time: 509 us -> 137 us (0.27)
  waiting for transfers between devices: 251 us -> 0 us
  matrix products: 195 us -> 0 us
  Pallas kernels: 0 us -> 135 us
  local copies, waits for them, and re-layouts: 25.6 us -> 1.28 us
  other arithmetic: 14.8 us -> 0 us
  between operations: 13.2 us -> 0.03 us
  starting transfers between devices: 6.94 us -> 0 us
    dot_general x48 -> x0, matrix products: 195 us -> none  [the longest x32 123 us: head_scores(): lax.dot_general(q_head, k_head, (((1,), (1,)), ((), ())), preferred_eleme...]
    pallas_call x0 -> x4, Pallas kernels: none -> 135 us  [the longest x1 56.3 us: gather(): pl.pallas_call(gather_kernel, out_shape=(shape, shape, jax.ShapeDtypeStru...]
    reduce_scatter x1 -> x0, waiting for transfers between devices: 114 us -> none  [sent_together(): lax.psum_scatter(both, axis, scatter_dimension=dim, tiled=True)]
    all_gather x3 -> x0, waiting for transfers between devices: 105 us -> none  [the longest x1 70.4 us: local(): lax.all_gather(normalize_rows(numer, totals), 'ka', axis=0, tiled=True)]
    all_to_all x1 -> x0, waiting for transfers between devices: 30.7 us -> none  [sent_to_all(): lax.all_to_all(jnp.broadcast_to(shard[None], (length, *shard.shape)), axi...]
    concatenate x1 -> x0, other arithmetic: 11.6 us -> none  [sent_together(): both = jnp.concatenate(arrays, axis=along)]
    broadcast_in_dim x2 -> x0, local copies, waits for them, and re-layouts: 9.45 us -> none  [the longest x1 7.89 us: local(): start_numer = jnp.zeros((query_rows, HEADS * HEAD_DIM), jnp.float32)]
    unnamed x1 -> x0, local copies, waits for them, and re-layouts: 8.44 us -> none
  transfers between devices with their start and end apart: 5 -> 0, of which waited for: 4 -> 0; matrix products, arithmetic and copies ran while one was open for 9% -> 0% of each run, Pallas kernels for 0% -> 0%
where the time goes in v1:
time: 137 us; the launch traced here: 136 us
  Pallas kernels  135 us (99%)
    pallas_call x1, Pallas kernels, gather(): pl.pallas_call(gather_kernel, out_shape=(shape, shape, jax.ShapeDtypeStru...  56.3 us
    pallas_call x1, Pallas kernels, spread(): pl.pallas_call(spread_kernel, out_shape=jax.ShapeDtypeStruct((NKA, ROWS,...  38.6 us
    pallas_call x1, Pallas kernels, attend(): pl.pallas_call(attend_kernel, out_shape=jax.ShapeDtypeStruct((NKA, ROWS,...  28.3 us
    pallas_call x1, Pallas kernels, weave(): pl.pallas_call(weave_kernel, out_shape=jax.ShapeDtypeStruct((ROWS, HEADS...  11.9 us

profile of v1, /device:TPU:0, one launch (start us, length us, event | category | flops | bytes accessed | tf_op | source)
XLA Modules:
  0.0 136.4 jit_solution(9175764276990661913)
XLA Ops:
  0.0 1.3 pad.4.m_ref
  1.3 56.3 %gather.1 = (bf16[8,16,128,128]{3,2,1,0:T(8,128)(2,1)}, bf16[8,16,128,128]{3,2,1,0:T(8,128)(2,1)}, s32[16,8,128]{2,1,0:T(8,128)}) custom-call(bf16[128,2048]{1,0:T(8,128)(2,1)} %k_ref.1, bf16[128,2048]{1,0:T(8,128)(2,1)} %v_ref.1, s32[8,128]{1,0:T(8,128)} %pad.4.m_ref), custom_call_target="tpu_custom_call" | custom-call | tf_op jit(solution)/shard_map/gather/pallas_call | solution.py:163
  57.6 28.3 %attend.1.in_ref = bf16[16,2048,128]{2,1,0:T(8,128)(2,1)} custom-call(bf16[2048,2048]{1,0:T(8,128)(2,1)} %q_hbm.1, bf16[8,16,128,128]{3,2,1,0:T(8,128)(2,1)} %get-tuple-element.8.k_hbm, bf16[8,16,128,128]{3,2,1,0:T(8,128)(2,1)} %get-tuple-element.9.v_hbm, s32[16,8,128]{2,1,0:T(8,128)} %get-tuple-element.10.m_ref), custom_call_target="tpu_custom_call" | custom-call | tf_op jit(solution)/shard_map/attend/pallas_call | solution.py:276
  85.9 38.6 %spread.1.in_ref = bf16[16,2048,128]{2,1,0:T(8,128)(2,1)} custom-call(bf16[16,2048,128]{2,1,0:T(8,128)(2,1)} %attend.1.in_ref), custom_call_target="tpu_custom_call", output_to_operand_aliasing={{}: (0, {})} | custom-call | tf_op jit(solution)/shard_map/spread/pallas_call | solution.py:385
  124.6 11.9 %weave.1 = bf16[2048,2048]{1,0:T(8,128)(2,1)} custom-call(bf16[16,2048,128]{2,1,0:T(8,128)(2,1)} %spread.1.in_ref), custom_call_target="tpu_custom_call" | custom-call | tf_op jit(solution)/shard_map/weave/pallas_call | solution.py:402

commit v2 on v0

v2 whole, which is shorter than its diff:
```python
import jax
import jax.numpy as jnp
from jax import lax
from jax.experimental import pallas as pl
from jax.experimental.pallas import tpu as pltpu
from jax.sharding import PartitionSpec as P

HEADS = 16
HEAD_DIM = 128
BLOCK = 128
NB = 128
NPB = 8
NKA = 16
ROWS = 2048
QBLOCKS = ROWS // BLOCK
SLOTS = 8
WAVE = HEAD_DIM // 2
PACKED = ROWS // 2
HALF = PACKED // 2
PIECE = PACKED // 4
DENSE = 2 * BLOCK
MESH = pl.DeviceIdType.MESH
BF16 = jnp.bfloat16
F32 = jnp.float32
SCALE = HEAD_DIM ** (-0.5) * 1.4426950408889634
NEG = -1e30


def remote(src, dst, send, recv, pb, ka):
    return pltpu.make_async_remote_copy(
        src_ref=src,
        dst_ref=dst,
        send_sem=send,
        recv_sem=recv,
        device_id={"pb": pb, "ka": ka},
        device_id_type=MESH,
    )


def greet(peers):
    barrier = pltpu.get_barrier_semaphore()
    for pb, ka in peers:
        pl.semaphore_signal(
            barrier, inc=1, device_id={"pb": pb, "ka": ka}, device_id_type=MESH
        )
    pl.semaphore_wait(barrier, len(peers))


def xor2(a, b):
    if b == 0:
        return a
    if b == 1:
        return a + 1 - 2 * (a % 2)
    if b == 2:
        return (a + 2) % 4
    return 3 - a


def nt(a, b):
    return lax.dot_general(a, b, (((1,), (1,)), ((), ())), preferred_element_type=F32)


def attend_kernel(
    q_hbm, k_hbm, v_hbm, m_hbm, out_ref,
    got, q_ref, v_own, vt_own, kb, vb0, vb1, mb, tab_v, tab_s, p_ref, tot_ref,
    sg, pg, mg, gtot, gacc,
    own_sem, a_send, a_recv, m_send, m_recv, z_send, z_recv, s_send, s_recv,
):
    pb = lax.axis_index("pb")
    ka = lax.axis_index("ka")
    other = pb + 1 - 2 * (pb % 2)
    up, down, far = (pb + 2) % NPB, (pb + 6) % NPB, (pb + 4) % NPB
    x, y = ka // 4, ka % 4
    vbs = (vb0, vb1)
    sends = []

    def cols(i):
        return pl.ds(pl.multiple_of(i * HEAD_DIM, HEAD_DIM), HEAD_DIM)

    vc = pltpu.make_async_copy(v_hbm, v_own, own_sem.at[0])
    vc.start()
    qc = pltpu.make_async_copy(q_hbm.at[:, cols(ka)], q_ref, own_sem.at[1])
    qc.start()
    kc = pltpu.make_async_copy(k_hbm.at[:, cols(ka)], kb.at[pb * NKA + ka], own_sem.at[2])
    kc.start()
    mc = pltpu.make_async_copy(m_hbm, mb.at[ka], own_sem.at[3])
    mc.start()

    peers = [xor2(x, d // 4) * 4 + xor2(y, d % 4) for d in range(NKA)]
    greet(
        [(pb, peers[d]) for d in range(1, NKA)] + [(other, ka), (up, ka), (down, ka)]
    )

    def begin(c):
        c.start()
        sends.append(c)

    for d in range(1, NKA):
        begin(remote(
            k_hbm.at[:, cols(peers[d])], kb.at[pb * NKA + ka],
            a_send.at[0, d], a_recv.at[0, d], pb, peers[d],
        ))
    for d in range(1, NKA):
        begin(remote(m_hbm, mb.at[ka], m_send.at[d], m_recv.at[d], pb, peers[d]))
    own_v = []

    def turn_values():
        vc.wait()
        for h in range(HEADS):
            tile = v_own[:, h * HEAD_DIM : (h + 1) * HEAD_DIM]
            vt_own[h * HEAD_DIM : (h + 1) * HEAD_DIM, :] = tile.T
        for w in range(2):
            def half(p, w=w):
                return pl.ds(pl.multiple_of(p * HEAD_DIM + w * WAVE, WAVE), WAVE)

            c = pltpu.make_async_copy(vt_own.at[half(ka)], vbs[w].at[pb * NKA + ka], own_sem.at[4 + w])
            c.start()
            own_v.append(c)
            for d in range(1, NKA):
                begin(remote(
                    vt_own.at[half(peers[d])], vbs[w].at[pb * NKA + ka],
                    a_send.at[1 + w, d], a_recv.at[1 + w, d], pb, peers[d],
                ))

    bufs = (kb, vb0, vb1)

    def group(buf, who, g, first=0, count=4):
        return buf.at[pl.ds(who * NKA + xor2(x, g) * 4 + first, count)]

    def send(kind, item, ref, to):
        begin(remote(ref, ref, z_send.at[kind, item], z_recv.at[kind, item], to, ka))

    def arrived(kind, item, ref):
        remote(ref, ref, z_send.at[kind, item], z_recv.at[kind, item], up, ka).wait_recv()

    def own(t):
        n, g = divmod(t, 4)
        if g == 0:
            (kc if n == 0 else own_v[n - 1]).wait()
        for d in range(4 * g, 4 * g + 4):
            if d:
                ref = bufs[n].at[pb * NKA + peers[d]]
                remote(ref, ref, a_send.at[n, d], a_recv.at[n, d], pb, ka).wait_recv()
        mine = group(bufs[n], pb, g)
        send(0, t, mine, up)
        send(1, t, mine, down)
        send(2, t, mine, other)

    def near(t):
        n, g = divmod(t, 4)
        low = group(bufs[n], down, g)
        arrived(0, t, low)
        send(3, t, group(bufs[n], down, g, 0, 2), up)
        send(5, t, low, other)
        high = group(bufs[n], up, g)
        arrived(1, t, high)
        send(4, t, group(bufs[n], up, g, 2, 2), down)
        send(6, t, high, other)

    def distant(t):
        n, g = divmod(t, 4)
        a = group(bufs[n], far, g, 0, 2)
        arrived(3, t, a)
        send(7, t, a, other)
        b = group(bufs[n], far, g, 2, 2)
        arrived(4, t, b)
        send(8, t, b, other)

    def relayed(t):
        n, g = divmod(t, 4)
        arrived(2, t, group(bufs[n], other, g))
        arrived(5, t, group(bufs[n], (other + 6) % NPB, g))
        arrived(6, t, group(bufs[n], (other + 2) % NPB, g))
        arrived(7, t, group(bufs[n], (other + 4) % NPB, g, 0, 2))
        arrived(8, t, group(bufs[n], (other + 4) % NPB, g, 2, 2))

    def make_table():
        mc.wait()
        for d in range(1, NKA):
            ref = mb.at[peers[d]]
            remote(ref, ref, m_send.at[d], m_recv.at[d], pb, ka).wait_recv()
        live = (mb[...].reshape(NB, 128) > 0).astype(F32)
        row = lax.broadcasted_iota(jnp.int32, (NB, 128), 0)
        col = lax.broadcasted_iota(jnp.int32, (NB, 128), 1)
        lower = (col <= row).astype(F32).astype(BF16)
        rank = jnp.dot(lower, live.astype(BF16), preferred_element_type=F32)
        weight = live * ((row % NPB) * NKA + row // NPB).astype(F32)
        parts = [
            jnp.sum(jnp.where(rank == s + 1, weight, 0.0), axis=0, keepdims=True)
            for s in range(SLOTS)
        ]
        count = jnp.sum(live, axis=0, keepdims=True)
        table = jnp.concatenate(parts + [jnp.broadcast_to(count, (8, 128))], axis=0)
        tab_v[...] = table.astype(jnp.int32)
        tc = pltpu.make_async_copy(tab_v, tab_s, own_sem.at[6])
        tc.start()
        tc.wait()

    def place(s, i):
        return jnp.minimum(jnp.maximum(tab_s[s, i], 0), NB - 1)

    def weigh(i, carry):
        q = q_ref[pl.ds(pl.multiple_of(i * BLOCK, BLOCK), BLOCK), :]
        n = tab_s[SLOTS, i]
        ss = []
        for s in range(SLOTS):
            k = kb[place(s, i)]
            ss.append(nt(q, k) * SCALE + jnp.where(s < n, 0.0, NEG))
        m = ss[0]
        for s in range(1, SLOTS):
            m = jnp.maximum(m, ss[s])
        m = jnp.max(m, axis=1, keepdims=True)
        total = None
        for s in range(SLOTS):
            p = jnp.exp2(ss[s] - m)
            total = p if total is None else total + p
            p_ref[i, s] = p.astype(BF16)
        tot_ref[i] = jnp.broadcast_to(jnp.sum(total, axis=1, keepdims=True), (BLOCK, 128))
        return carry

    def gathered(w, i):
        out = None
        for s in range(SLOTS):
            o = nt(p_ref[i, s], vbs[w][place(s, i)])
            out = o if out is None else out + o
        return out / tot_ref[i, :, :WAVE]

    def value(w):
        def pair(i, carry):
            o = jnp.concatenate([gathered(w, i), gathered(w, i + 8)], axis=1)
            got[w, ka, pl.ds(pl.multiple_of(i * BLOCK, BLOCK), BLOCK), :] = o.astype(BF16)
            return carry

        lax.fori_loop(0, QBLOCKS // 2, pair, 0)

        @pl.when(pb == 0)
        def _():
            dense = (gacc[w] / gtot[...])[:, :WAVE].astype(BF16)
            right = got[w, ka, 0:DENSE, WAVE:]
            got[w, ka, 0:DENSE, :] = jnp.concatenate([dense, right], axis=1)

    def dense_weigh(g):
        @pl.when(pb == 0)
        def _():
            q = q_ref[0:DENSE, :]
            base = xor2(x, g) * 4

            def score(b, m):
                k = kb[pl.ds(b * NKA + base, 4)].reshape(4 * BLOCK, HEAD_DIM)
                s = nt(q, k) * SCALE
                sg[b] = s
                for j in range(4):
                    m = jnp.maximum(m, s[:, j * 128 : (j + 1) * 128])
                return m

            old = mg[g - 1] if g else jnp.full((DENSE, 128), NEG, F32)
            m = lax.fori_loop(0, NPB, score, old)
            m = jnp.broadcast_to(jnp.max(m, axis=1, keepdims=True), (DENSE, 128))
            mg[g] = m

            def expo(b, total):
                for j in range(4):
                    p = jnp.exp2(sg[b, :, j * 128 : (j + 1) * 128] - mg[g])
                    total = total + p
                    pg[g, b, :, j * 128 : (j + 1) * 128] = p.astype(BF16)
                return total

            total = lax.fori_loop(0, NPB, expo, jnp.zeros((DENSE, 128), F32))
            total = jnp.broadcast_to(jnp.sum(total, axis=1, keepdims=True), (DENSE, 128))
            gtot[...] = total + gtot[...] * jnp.exp2(old - m) if g else total

    def dense_value(w, g):
        @pl.when(pb == 0)
        def _():
            base = xor2(x, g) * 4

            def part(b, acc):
                v = vbs[w][pl.ds(b * NKA + base, 4)]
                v = jnp.concatenate([v[j] for j in range(4)], axis=1)
                return acc + nt(pg[g, b], v)

            acc = lax.fori_loop(0, NPB, part, jnp.zeros((DENSE, WAVE), F32))
            acc = acc * jnp.exp2(mg[g] - mg[3])[:, :WAVE]
            acc = jnp.concatenate([acc, acc], axis=1)
            gacc[w] = gacc[w] + acc if g else acc

    def at(dx, dy):
        return ((x + dx + 4) % 4) * 4 + (y + dy + 4) % 4

    class Spread:
        def __init__(self, wave):
            self.wave = wave

        def place(self, a, u, w):
            return at(u, w) if a == 0 else at(w, u)

        def ref(self, a, u, w, piece):
            lo, n = (0, 2) if piece is None else (piece, 1)
            return got.at[
                self.wave, self.place(a, u, w), pl.ds(a * HALF + lo * PIECE, n * PIECE)
            ]

        def sem_id(self, u, w, piece):
            return ((u % 4) * 4 + w % 4) * 3 + (2 if piece is None else piece)

        def send(self, a, u, w, piece, du, dw):
            i = self.sem_id(u - du, w - dw, piece)
            r = self.ref(a, u, w, piece)
            begin(remote(
                r, r, s_send.at[self.wave, a, i], s_recv.at[self.wave, a, i],
                pb, self.place(a, du, dw),
            ))

        def arrived(self, a, u, w, piece):
            i = self.sem_id(u, w, piece)
            r = self.ref(a, u, w, piece)
            remote(
                r, r, s_send.at[self.wave, a, i], s_recv.at[self.wave, a, i], pb, ka
            ).wait_recv()

        def stage(self, n):
            send, arrived = self.send, self.arrived
            both = (0, 1)
            if n == 0:
                for a in both:
                    send(a, 0, 0, None, 1, 0)
                    send(a, 0, 0, None, -1, 0)
                for a in both:
                    send(a, 0, 0, None, 0, 1)
                    send(a, 0, 0, None, 0, -1)
            elif n == 1:
                for a in both:
                    arrived(a, -1, 0, None)
                    send(a, -1, 0, 0, 1, 0)
                    arrived(a, 1, 0, None)
                    send(a, 1, 0, 1, -1, 0)
                for a in both:
                    for u in (-1, 1):
                        send(a, u, 0, None, 0, 1)
                        send(a, u, 0, None, 0, -1)
            elif n == 2:
                for a in both:
                    arrived(a, 0, -1, None)
                    send(a, 0, -1, 0, 0, 1)
                    arrived(a, 0, 1, None)
                    send(a, 0, 1, 1, 0, -1)
            elif n == 3:
                for a in both:
                    for piece in (0, 1):
                        arrived(a, 2, 0, piece)
                        send(a, 2, 0, piece, 0, 1)
                        send(a, 2, 0, piece, 0, -1)
            elif n == 4:
                for u in (-1, 1):
                    for a in both:
                        arrived(a, u, -1, None)
                        send(a, u, -1, 0, 0, 1)
                        arrived(a, u, 1, None)
                        send(a, u, 1, 1, 0, -1)
            elif n == 5:
                for a in both:
                    arrived(a, 2, -1, 0)
                    send(a, 2, -1, 0, 0, 1)
                    arrived(a, 2, 1, 0)
                for a in both:
                    arrived(a, 2, 1, 1)
                    send(a, 2, 1, 1, 0, -1)
                    arrived(a, 2, -1, 1)
            else:
                for a in both:
                    for u in (0, -1, 1, 2):
                        for piece in (0, 1):
                            arrived(a, u, 2, piece)

    def unpack(a, u, w, piece):
        h = first.place(a, u, w)
        lo, n = (0, 2) if piece is None else (piece, 1)
        lanes = pl.ds(pl.multiple_of(h * HEAD_DIM, HEAD_DIM), HEAD_DIM)

        def rows(r, carry):
            at_row = a * HALF + lo * PIECE + r * BLOCK
            src = pl.ds(pl.multiple_of(at_row, BLOCK), BLOCK)
            low, high = got[0, h, src, :], got[1, h, src, :]
            out_ref[src, lanes] = jnp.concatenate([low[:, :WAVE], high[:, :WAVE]], axis=1)
            dst = pl.ds(pl.multiple_of(PACKED + at_row, BLOCK), BLOCK)
            out_ref[dst, lanes] = jnp.concatenate([low[:, WAVE:], high[:, WAVE:]], axis=1)
            return carry

        lax.fori_loop(0, n * PIECE // BLOCK, rows, 0)

    both = (0, 1)
    first, second = Spread(0), Spread(1)
    own(0)
    own(1)
    turn_values()
    own(2)
    near(0)
    qc.wait()
    make_table()
    own(3)
    for t in range(4):
        near(t + 1)
        distant(t)
        relayed(t)
        if t < 3:
            own(t + 4)
        dense_weigh(t)
    lax.fori_loop(0, 3, weigh, 0)
    own(7)
    near(5)
    distant(4)
    relayed(4)
    dense_value(0, 0)
    lax.fori_loop(3, 6, weigh, 0)
    near(6)
    distant(5)
    relayed(5)
    dense_value(0, 1)
    lax.fori_loop(6, 9, weigh, 0)
    near(7)
    own(8)
    distant(6)
    relayed(6)
    dense_value(0, 2)
    lax.fori_loop(9, 12, weigh, 0)
    distant(7)
    own(9)
    lax.fori_loop(12, 16, weigh, 0)
    relayed(7)
    dense_value(0, 3)
    value(0)
    first.stage(0)
    near(8)
    own(10)
    near(9)
    distant(8)
    relayed(8)
    dense_value(1, 0)
    own(11)
    first.stage(1)
    near(10)
    distant(9)
    relayed(9)
    dense_value(1, 1)
    near(11)
    distant(10)
    relayed(10)
    dense_value(1, 2)
    first.stage(2)
    distant(11)
    relayed(11)
    dense_value(1, 3)
    value(1)
    second.stage(0)
    for a in both:
        unpack(a, 0, 0, None)
    first.stage(3)
    first.stage(4)
    second.stage(1)
    for a in both:
        unpack(a, -1, 0, None)
        unpack(a, 1, 0, None)
    first.stage(5)
    second.stage(2)
    for a in both:
        unpack(a, 0, -1, None)
        unpack(a, 0, 1, None)
    first.stage(6)
    second.stage(3)
    for a in both:
        unpack(a, 2, 0, None)
    second.stage(4)
    for a in both:
        for u in (-1, 1):
            unpack(a, u, -1, None)
            unpack(a, u, 1, None)
    second.stage(5)
    for a in both:
        unpack(a, 2, -1, None)
        unpack(a, 2, 1, None)
    for u in (0, -1, 1, 2):
        for a in both:
            for piece in (0, 1):
                second.arrived(a, u, 2, piece)
                unpack(a, u, 2, piece)
    for c in sends:
        c.wait_send()


def attend(queries, keys, values, mask_t):
    any_spec = pl.BlockSpec(memory_space=pltpu.HBM)
    dma = pltpu.SemaphoreType.DMA
    vmem = pltpu.VMEM
    return pl.pallas_call(
        attend_kernel,
        out_shape=pltpu.VMEM((ROWS, HEADS * HEAD_DIM), BF16),
        in_specs=[any_spec] * 4,
        out_specs=pl.BlockSpec(memory_space=pltpu.VMEM),
        scratch_shapes=[
            vmem((2, NKA, PACKED, 128), BF16),
            vmem((ROWS, HEAD_DIM), BF16),
            vmem((BLOCK, HEADS * HEAD_DIM), BF16),
            vmem((HEADS * HEAD_DIM, BLOCK), BF16),
            vmem((NB, BLOCK, HEAD_DIM), BF16),
            vmem((NB, WAVE, BLOCK), BF16),
            vmem((NB, WAVE, BLOCK), BF16),
            vmem((NKA, 8, 128), jnp.int32),
            vmem((16, 128), jnp.int32),
            pltpu.SMEM((16, 128), jnp.int32),
            vmem((QBLOCKS, SLOTS, BLOCK, BLOCK), BF16),
            vmem((QBLOCKS, BLOCK, 128), F32),
            vmem((NPB, DENSE, 4 * BLOCK), F32),
            vmem((4, NPB, DENSE, 4 * BLOCK), BF16),
            vmem((4, DENSE, 128), F32),
            vmem((DENSE, 128), F32),
            vmem((2, DENSE, 128), F32),
            dma((7,)), dma((3, NKA)), dma((3, NKA)), dma((NKA,)), dma((NKA,)),
            dma((9, 12)), dma((9, 12)), dma((2, 2, 48)), dma((2, 2, 48)),
        ],
        compiler_params=pltpu.CompilerParams(
            collective_id=0, has_side_effects=True, vmem_limit_bytes=58_400_000
        ),
        name="attend",
    )(queries, keys, values, mask_t)


def local(queries, keys, values, block_mask):
    mask_t = jnp.pad(block_mask.T, ((0, 0), (0, 112)))
    return attend(queries, keys, values, mask_t)


def solution(mesh):
    return jax.shard_map(
        local,
        mesh=mesh,
        in_specs=(P("pb", None), P(("ka", "pb"), None), P(("ka", "pb"), None), P("pb", "ka")),
        out_specs=P("pb", None),
        check_vma=False,
    )
```

time: 509 us -> 121 us (0.24)
  waiting for transfers between devices: 251 us -> 0 us
  matrix products: 195 us -> 0 us
  Pallas kernels: 0 us -> 116 us
  local copies, waits for them, and re-layouts: 25.6 us -> 4.68 us
  other arithmetic: 14.8 us -> 0 us
  between operations: 13.2 us -> 0.01 us
  starting transfers between devices: 6.94 us -> 0 us
    dot_general x48 -> x0, matrix products: 195 us -> none  [the longest x32 123 us: head_scores(): lax.dot_general(q_head, k_head, (((1,), (1,)), ((), ())), preferred_eleme...]
    pallas_call x0 -> x1, Pallas kernels: none -> 116 us  [attend(): pl.pallas_call(attend_kernel, out_shape=pltpu.VMEM((ROWS, HEADS * HEAD_DI...]
    reduce_scatter x1 -> x0, waiting for transfers between devices: 114 us -> none  [sent_together(): lax.psum_scatter(both, axis, scatter_dimension=dim, tiled=True)]
    all_gather x3 -> x0, waiting for transfers between devices: 105 us -> none  [the longest x1 70.4 us: local(): lax.all_gather(normalize_rows(numer, totals), 'ka', axis=0, tiled=True)]
    all_to_all x1 -> x0, waiting for transfers between devices: 30.7 us -> none  [sent_to_all(): lax.all_to_all(jnp.broadcast_to(shard[None], (length, *shard.shape)), axi...]
    concatenate x1 -> x0, other arithmetic: 11.6 us -> none  [sent_together(): both = jnp.concatenate(arrays, axis=along)]
    broadcast_in_dim x2 -> x0, local copies, waits for them, and re-layouts: 9.45 us -> none  [the longest x1 7.89 us: local(): start_numer = jnp.zeros((query_rows, HEADS * HEAD_DIM), jnp.float32)]
    all_to_all x1 -> x0, starting transfers between devices: 6.82 us -> none  [sent_to_all(): lax.all_to_all(jnp.broadcast_to(shard[None], (length, *shard.shape)), axi...]
  transfers between devices with their start and end apart: 5 -> 0, of which waited for: 4 -> 0; matrix products, arithmetic and copies ran while one was open for 9% -> 0% of each run, Pallas kernels for 0% -> 0%
where the time goes in v2:
time: 121 us
  Pallas kernels  116 us (96%)
  local copies, waits for them, and re-layouts  4.68 us (4%)
    pallas_call x1, Pallas kernels, attend(): pl.pallas_call(attend_kernel, out_shape=pltpu.VMEM((ROWS, HEADS * HEAD_DI...  116 us
    unnamed x1, local copies, waits for them, and re-layouts  3.4 us

profile of v2, /device:TPU:0, one launch (start us, length us, event | category | flops | bytes accessed | tf_op | source)
XLA Modules:
  0.0 121.0 jit_solution(3191469329323923534)
XLA Ops:
  0.0 1.3 %pad.4.m_hbm = s32[8,128]{1,0:T(8,128)} pad(s32[8,16]{1,0:T(8,128)} %bitcast.1, s32[]{:T(128)} %constant.0.clone.1), padding=0_0x0_112 | pad | bytes 4612 | tf_op jit(solution)/shard_map/jit(_pad)/pad | solution.py:528
  1.3 116.3 %attend.1 = bf16[2048,2048]{1,0:T(8,128)(2,1)S(1)} custom-call(bf16[2048,2048]{1,0:T(8,128)(2,1)} %q_hbm.1, bf16[128,2048]{1,0:T(8,128)(2,1)} %k_hbm.1, bf16[128,2048]{1,0:T(8,128)(2,1)} %v_hbm.1, s32[8,128]{1,0:T(8,128)} %pad.4.m_hbm), custom_call_target="tpu_custom_call" | custom-call | tf_op jit(solution)/shard_map/attend/pallas_call | solution.py:494
  117.6 3.4 %copy.6 = bf16[2048,2048]{1,0:T(8,128)(2,1)} copy(bf16[2048,2048]{1,0:T(8,128)(2,1)S(1)} %attend.1) | data formatting | bytes 16777216

commit v3 on v2

--- a/solution.py
+++ b/solution.py
@@ -64,7 +64,7 @@
     q_hbm, k_hbm, v_hbm, m_hbm, out_ref,
     got, q_ref, v_own, vt_own, kb, vb0, vb1, mb, tab_v, tab_s, p_ref, tot_ref,
     sg, pg, mg, gtot, gacc,
-    own_sem, a_send, a_recv, m_send, m_recv, z_send, z_recv, s_send, s_recv,
+    sem, a_recv, z_send, z_recv, s_send, s_recv,
 ):
     pb = lax.axis_index("pb")
     ka = lax.axis_index("ka")
@@ -72,37 +72,33 @@
     up, down, far = (pb + 2) % NPB, (pb + 6) % NPB, (pb + 4) % NPB
     x, y = ka // 4, ka % 4
     vbs = (vb0, vb1)
-    sends = []
 
     def cols(i):
         return pl.ds(pl.multiple_of(i * HEAD_DIM, HEAD_DIM), HEAD_DIM)
 
-    vc = pltpu.make_async_copy(v_hbm, v_own, own_sem.at[0])
+    vc = pltpu.make_async_copy(v_hbm, v_own, sem.at[0])
     vc.start()
-    qc = pltpu.make_async_copy(q_hbm.at[:, cols(ka)], q_ref, own_sem.at[1])
-    qc.start()
-    kc = pltpu.make_async_copy(k_hbm.at[:, cols(ka)], kb.at[pb * NKA + ka], own_sem.at[2])
-    kc.start()
-    mc = pltpu.make_async_copy(m_hbm, mb.at[ka], own_sem.at[3])
-    mc.start()
+    qc = pltpu.make_async_copy(q_hbm.at[:, cols(ka)], q_ref, sem.at[1])
+    pltpu.make_async_copy(k_hbm.at[:, cols(ka)], kb.at[pb * NKA + ka], a_recv.at[0]).start()
+    pltpu.make_async_copy(m_hbm, mb.at[ka], sem.at[3]).start()
 
     peers = [xor2(x, d // 4) * 4 + xor2(y, d % 4) for d in range(NKA)]
     greet(
         [(pb, peers[d]) for d in range(1, NKA)] + [(other, ka), (up, ka), (down, ka)]
     )
 
-    def begin(c):
-        c.start()
-        sends.append(c)
-
-    for d in range(1, NKA):
-        begin(remote(
-            k_hbm.at[:, cols(peers[d])], kb.at[pb * NKA + ka],
-            a_send.at[0, d], a_recv.at[0, d], pb, peers[d],
-        ))
-    for d in range(1, NKA):
-        begin(remote(m_hbm, mb.at[ka], m_send.at[d], m_recv.at[d], pb, peers[d]))
-    own_v = []
+    def take(s, ref):
+        remote(ref, ref, s, s, pb, ka).wait_recv()
+
+    def half(p, w):
+        return pl.ds(pl.multiple_of(p * HEAD_DIM + w * WAVE, WAVE), WAVE)
+
+    def exchange(n, g):
+        for d in range(4 * g, 4 * g + 4):
+            if d:
+                src = vt_own.at[half(peers[d], n - 1)] if n else k_hbm.at[:, cols(peers[d])]
+                dst = (kb, vb0, vb1)[n].at[pb * NKA + ka]
+                remote(src, dst, sem.at[5 + n], a_recv.at[n * 4 + g], pb, peers[d]).start()
 
     def turn_values():
         vc.wait()
@@ -110,75 +106,53 @@
             tile = v_own[:, h * HEAD_DIM : (h + 1) * HEAD_DIM]
             vt_own[h * HEAD_DIM : (h + 1) * HEAD_DIM, :] = tile.T
         for w in range(2):
-            def half(p, w=w):
-                return pl.ds(pl.multiple_of(p * HEAD_DIM + w * WAVE, WAVE), WAVE)
-
-            c = pltpu.make_async_copy(vt_own.at[half(ka)], vbs[w].at[pb * NKA + ka], own_sem.at[4 + w])
-            c.start()
-            own_v.append(c)
-            for d in range(1, NKA):
-                begin(remote(
-                    vt_own.at[half(peers[d])], vbs[w].at[pb * NKA + ka],
-                    a_send.at[1 + w, d], a_recv.at[1 + w, d], pb, peers[d],
-                ))
+            pltpu.make_async_copy(
+                vt_own.at[half(ka, w)], vbs[w].at[pb * NKA + ka], a_recv.at[4 + 4 * w]
+            ).start()
+
+    exchange(0, 0)
+    exchange(0, 1)
+    for d in range(1, NKA):
+        remote(m_hbm, mb.at[ka], sem.at[4], sem.at[3], pb, peers[d]).start()
+    qc.start()
 
     bufs = (kb, vb0, vb1)
 
     def group(buf, who, g, first=0, count=4):
         return buf.at[pl.ds(who * NKA + xor2(x, g) * 4 + first, count)]
 
-    def send(kind, item, ref, to):
-        begin(remote(ref, ref, z_send.at[kind, item], z_recv.at[kind, item], to, ka))
-
-    def arrived(kind, item, ref):
-        remote(ref, ref, z_send.at[kind, item], z_recv.at[kind, item], up, ka).wait_recv()
+    NEAR, DISTANT, RELAYED = 0, 12, 24
+
+    def send(t, kind, ref, to):
+        remote(ref, ref, z_send.at[t // 4], z_recv.at[kind + t], to, ka).start()
 
     def own(t):
         n, g = divmod(t, 4)
-        if g == 0:
-            (kc if n == 0 else own_v[n - 1]).wait()
-        for d in range(4 * g, 4 * g + 4):
-            if d:
-                ref = bufs[n].at[pb * NKA + peers[d]]
-                remote(ref, ref, a_send.at[n, d], a_recv.at[n, d], pb, ka).wait_recv()
         mine = group(bufs[n], pb, g)
-        send(0, t, mine, up)
-        send(1, t, mine, down)
-        send(2, t, mine, other)
+        take(a_recv.at[t], mine)
+        send(t, NEAR, mine, up)
+        send(t, NEAR, mine, down)
+        send(t, RELAYED, mine, other)
 
     def near(t):
         n, g = divmod(t, 4)
-        low = group(bufs[n], down, g)
-        arrived(0, t, low)
-        send(3, t, group(bufs[n], down, g, 0, 2), up)
-        send(5, t, low, other)
-        high = group(bufs[n], up, g)
-        arrived(1, t, high)
-        send(4, t, group(bufs[n], up, g, 2, 2), down)
-        send(6, t, high, other)
+        take(z_recv.at[NEAR + t], bufs[n].at[pl.ds(0, 8)])
+        send(t, DISTANT, group(bufs[n], down, g, 0, 2), up)
+        send(t, DISTANT, group(bufs[n], up, g, 2, 2), down)
+        send(t, RELAYED, group(bufs[n], down, g), other)
+        send(t, RELAYED, group(bufs[n], up, g), other)
 
     def distant(t):
         n, g = divmod(t, 4)
-        a = group(bufs[n], far, g, 0, 2)
-        arrived(3, t, a)
-        send(7, t, a, other)
-        b = group(bufs[n], far, g, 2, 2)
-        arrived(4, t, b)
-        send(8, t, b, other)
+        both = group(bufs[n], far, g)
+        take(z_recv.at[DISTANT + t], both)
+        send(t, RELAYED, both, other)
 
     def relayed(t):
-        n, g = divmod(t, 4)
-        arrived(2, t, group(bufs[n], other, g))
-        arrived(5, t, group(bufs[n], (other + 6) % NPB, g))
-        arrived(6, t, group(bufs[n], (other + 2) % NPB, g))
-        arrived(7, t, group(bufs[n], (other + 4) % NPB, g, 0, 2))
-        arrived(8, t, group(bufs[n], (other + 4) % NPB, g, 2, 2))
+        take(z_recv.at[RELAYED + t], bufs[t // 4].at[pl.ds(0, 16)])
 
     def make_table():
-        mc.wait()
-        for d in range(1, NKA):
-            ref = mb.at[peers[d]]
-            remote(ref, ref, m_send.at[d], m_recv.at[d], pb, ka).wait_recv()
+        take(sem.at[3], mb)
         live = (mb[...].reshape(NB, 128) > 0).astype(F32)
         row = lax.broadcasted_iota(jnp.int32, (NB, 128), 0)
         col = lax.broadcasted_iota(jnp.int32, (NB, 128), 1)
@@ -192,7 +166,7 @@
         count = jnp.sum(live, axis=0, keepdims=True)
         table = jnp.concatenate(parts + [jnp.broadcast_to(count, (8, 128))], axis=0)
         tab_v[...] = table.astype(jnp.int32)
-        tc = pltpu.make_async_copy(tab_v, tab_s, own_sem.at[6])
+        tc = pltpu.make_async_copy(tab_v, tab_s, sem.at[2])
         tc.start()
         tc.wait()
 
@@ -300,23 +274,26 @@
                 self.wave, self.place(a, u, w), pl.ds(a * HALF + lo * PIECE, n * PIECE)
             ]
 
-        def sem_id(self, u, w, piece):
-            return ((u % 4) * 4 + w % 4) * 3 + (2 if piece is None else piece)
+        def place_id(self, u, w):
+            u, w = u % 4, w % 4
+            if w == 2:
+                return 6 + u
+            if w == 0:
+                return 2 if u == 2 else 0
+            return {0: 1, 3: 3, 1: 4, 2: 5}[u]
 
         def send(self, a, u, w, piece, du, dw):
-            i = self.sem_id(u - du, w - dw, piece)
             r = self.ref(a, u, w, piece)
-            begin(remote(
-                r, r, s_send.at[self.wave, a, i], s_recv.at[self.wave, a, i],
+            i = self.place_id(u - du, w - dw)
+            remote(
+                r, r, s_send.at[self.wave], s_recv.at[self.wave, i],
                 pb, self.place(a, du, dw),
-            ))
-
-        def arrived(self, a, u, w, piece):
-            i = self.sem_id(u, w, piece)
-            r = self.ref(a, u, w, piece)
-            remote(
-                r, r, s_send.at[self.wave, a, i], s_recv.at[self.wave, a, i], pb, ka
-            ).wait_recv()
+            ).start()
+
+        def arrived(self, u, w):
+            i = self.place_id(u, w)
+            heads = {0: 2, 1: 2, 2: 1, 3: 2, 4: 2, 5: 2}.get(i, 1)
+            take(s_recv.at[self.wave, i], got.at[self.wave, pl.ds(0, heads)])
 
         def stage(self, n):
             send, arrived = self.send, self.arrived
@@ -329,48 +306,39 @@
                     send(a, 0, 0, None, 0, 1)
                     send(a, 0, 0, None, 0, -1)
             elif n == 1:
-                for a in both:
-                    arrived(a, -1, 0, None)
+                arrived(1, 0)
+                for a in both:
                     send(a, -1, 0, 0, 1, 0)
-                    arrived(a, 1, 0, None)
                     send(a, 1, 0, 1, -1, 0)
                 for a in both:
                     for u in (-1, 1):
                         send(a, u, 0, None, 0, 1)
                         send(a, u, 0, None, 0, -1)
             elif n == 2:
-                for a in both:
-                    arrived(a, 0, -1, None)
+                arrived(0, 1)
+                for a in both:
                     send(a, 0, -1, 0, 0, 1)
-                    arrived(a, 0, 1, None)
                     send(a, 0, 1, 1, 0, -1)
             elif n == 3:
+                arrived(2, 0)
                 for a in both:
                     for piece in (0, 1):
-                        arrived(a, 2, 0, piece)
                         send(a, 2, 0, piece, 0, 1)
                         send(a, 2, 0, piece, 0, -1)
             elif n == 4:
                 for u in (-1, 1):
+                    arrived(u, 1)
                     for a in both:
-                        arrived(a, u, -1, None)
                         send(a, u, -1, 0, 0, 1)
-                        arrived(a, u, 1, None)
                         send(a, u, 1, 1, 0, -1)
             elif n == 5:
-                for a in both:
-                    arrived(a, 2, -1, 0)
+                arrived(2, 1)
+                for a in both:
                     send(a, 2, -1, 0, 0, 1)
-                    arrived(a, 2, 1, 0)
-                for a in both:
-                    arrived(a, 2, 1, 1)
                     send(a, 2, 1, 1, 0, -1)
-                    arrived(a, 2, -1, 1)
             else:
-                for a in both:
-                    for u in (0, -1, 1, 2):
-                        for piece in (0, 1):
-                            arrived(a, u, 2, piece)
+                for u in (0, -1, 1, 2):
+                    arrived(u, 2)
 
     def unpack(a, u, w, piece):
         h = first.place(a, u, w)
@@ -391,20 +359,40 @@
     both = (0, 1)
     first, second = Spread(0), Spread(1)
     own(0)
+    exchange(0, 2)
     own(1)
+    exchange(0, 3)
     turn_values()
+    near(0)
     own(2)
-    near(0)
+    exchange(1, 0)
+    exchange(1, 1)
+    near(1)
+    own(3)
+    exchange(1, 2)
+    exchange(1, 3)
+    distant(0)
+    relayed(0)
     qc.wait()
+    dense_weigh(0)
+    near(2)
+    distant(1)
+    for g in range(4):
+        exchange(2, g)
+    own(4)
     make_table()
-    own(3)
-    for t in range(4):
-        near(t + 1)
-        distant(t)
-        relayed(t)
-        if t < 3:
-            own(t + 4)
-        dense_weigh(t)
+    relayed(1)
+    near(3)
+    own(5)
+    dense_weigh(1)
+    distant(2)
+    relayed(2)
+    near(4)
+    own(6)
+    dense_weigh(2)
+    distant(3)
+    relayed(3)
+    dense_weigh(3)
     lax.fori_loop(0, 3, weigh, 0)
     own(7)
     near(5)
@@ -479,12 +467,21 @@
         unpack(a, 2, -1, None)
         unpack(a, 2, 1, None)
     for u in (0, -1, 1, 2):
+        second.arrived(u, 2)
         for a in both:
-            for piece in (0, 1):
-                second.arrived(a, u, 2, piece)
-                unpack(a, u, 2, piece)
-    for c in sends:
-        c.wait_send()
+            unpack(a, u, 2, None)
+    for s, ref in (
+        (sem.at[4], mb.at[pl.ds(0, NKA - 1)]),
+        (sem.at[5], kb.at[pl.ds(0, NKA - 1)]),
+        (sem.at[6], vb0.at[pl.ds(0, NKA - 1)]),
+        (sem.at[7], vb1.at[pl.ds(0, NKA - 1)]),
+        (z_send.at[0], kb.at[pl.ds(0, 112)]),
+        (z_send.at[1], vb0.at[pl.ds(0, 112)]),
+        (z_send.at[2], vb1.at[pl.ds(0, 112)]),
+        (s_send.at[0], got.at[0, pl.ds(0, NKA - 1)]),
+        (s_send.at[1], got.at[1, pl.ds(0, NKA - 1)]),
+    ):
+        remote(ref, ref, s, s, pb, ka).wait_send()
 
 
 def attend(queries, keys, values, mask_t):
@@ -514,8 +511,7 @@
             vmem((4, DENSE, 128), F32),
             vmem((DENSE, 128), F32),
             vmem((2, DENSE, 128), F32),
-            dma((7,)), dma((3, NKA)), dma((3, NKA)), dma((NKA,)), dma((NKA,)),
-            dma((9, 12)), dma((9, 12)), dma((2, 2, 48)), dma((2, 2, 48)),
+            dma((8,)), dma((12,)), dma((3,)), dma((36,)), dma((2,)), dma((2, 10)),
         ],
         compiler_params=pltpu.CompilerParams(
             collective_id=0, has_side_effects=True, vmem_limit_bytes=58_400_000

time: 121 us -> 112 us (0.926)
  Pallas kernels: 116 us -> 107 us
    pallas_call x1, Pallas kernels: 116 us -> 107 us  [attend(): pl.pallas_call(attend_kernel, out_shape=pltpu.VMEM((ROWS, HEADS * HEAD_DI...]
where the time goes in v3:
time: 112 us
  Pallas kernels  107 us (96%)
  local copies, waits for them, and re-layouts  4.68 us (4%)
    pallas_call x1, Pallas kernels, attend(): pl.pallas_call(attend_kernel, out_shape=pltpu.VMEM((ROWS, HEADS * HEAD_DI...  107 us
    unnamed x1, local copies, waits for them, and re-layouts  3.4 us

profile of v3, /device:TPU:0, one launch (start us, length us, event | category | flops | bytes accessed | tf_op | source)
XLA Modules:
  0.0 112.1 jit_solution(16702815230424197853)
XLA Ops:
  0.0 1.3 %pad.4.m_hbm = s32[8,128]{1,0:T(8,128)} pad(s32[8,16]{1,0:T(8,128)} %bitcast.1, s32[]{:T(128)} %constant.0.clone.1), padding=0_0x0_112 | pad | bytes 4612 | tf_op jit(solution)/shard_map/jit(_pad)/pad | solution.py:524
  1.3 107.4 %attend.1 = bf16[2048,2048]{1,0:T(8,128)(2,1)S(1)} custom-call(bf16[2048,2048]{1,0:T(8,128)(2,1)} %q_hbm.1, bf16[128,2048]{1,0:T(8,128)(2,1)} %k_hbm.1, bf16[128,2048]{1,0:T(8,128)(2,1)} %v_hbm.1, s32[8,128]{1,0:T(8,128)} %pad.4.m_hbm), custom_call_target="tpu_custom_call" | custom-call | tf_op jit(solution)/shard_map/attend/pallas_call | solution.py:491
  108.7 3.4 %copy.6 = bf16[2048,2048]{1,0:T(8,128)(2,1)} copy(bf16[2048,2048]{1,0:T(8,128)(2,1)S(1)} %attend.1) | data formatting | bytes 16777216

commit v4 on v3

--- a/solution.py
+++ b/solution.py
@@ -178,40 +178,42 @@
         n = tab_s[SLOTS, i]
         ss = []
         for s in range(SLOTS):
-            k = kb[place(s, i)]
-            ss.append(nt(q, k) * SCALE + jnp.where(s < n, 0.0, NEG))
+            ss.append(nt(kb[place(s, i)], q) * SCALE + jnp.where(s < n, 0.0, NEG))
         m = ss[0]
         for s in range(1, SLOTS):
             m = jnp.maximum(m, ss[s])
-        m = jnp.max(m, axis=1, keepdims=True)
+        m = jnp.max(m, axis=0, keepdims=True)
         total = None
         for s in range(SLOTS):
             p = jnp.exp2(ss[s] - m)
             total = p if total is None else total + p
             p_ref[i, s] = p.astype(BF16)
-        tot_ref[i] = jnp.broadcast_to(jnp.sum(total, axis=1, keepdims=True), (BLOCK, 128))
+        tot_ref[i] = jnp.broadcast_to(jnp.sum(total, axis=0, keepdims=True), (8, 128))
         return carry
 
     def gathered(w, i):
-        out = None
-        for s in range(SLOTS):
-            o = nt(p_ref[i, s], vbs[w][place(s, i)])
-            out = o if out is None else out + o
-        return out / tot_ref[i, :, :WAVE]
+        v = jnp.concatenate([vbs[w][place(s, i)] for s in range(SLOTS)], axis=1)
+        p = p_ref[i].reshape(SLOTS * BLOCK, BLOCK)
+        return jnp.dot(v, p, preferred_element_type=F32) / tot_ref[i, 0:1, :]
 
     def value(w):
         def pair(i, carry):
-            o = jnp.concatenate([gathered(w, i), gathered(w, i + 8)], axis=1)
-            got[w, ka, pl.ds(pl.multiple_of(i * BLOCK, BLOCK), BLOCK), :] = o.astype(BF16)
+            o = jnp.concatenate([gathered(w, i), gathered(w, i + 8)], axis=0)
+            got[w, ka, pl.ds(pl.multiple_of(i * BLOCK, BLOCK), BLOCK), :] = o.T.astype(BF16)
             return carry
 
         lax.fori_loop(0, QBLOCKS // 2, pair, 0)
 
         @pl.when(pb == 0)
         def _():
-            dense = (gacc[w] / gtot[...])[:, :WAVE].astype(BF16)
-            right = got[w, ka, 0:DENSE, WAVE:]
-            got[w, ka, 0:DENSE, :] = jnp.concatenate([dense, right], axis=1)
+            dense = gacc[w] / gtot[0:1, :]
+            for i in range(2):
+                o = dense[:, i * BLOCK : (i + 1) * BLOCK]
+                o = jnp.concatenate([o, o], axis=0).T.astype(BF16)
+                right = got[w, ka, i * BLOCK : (i + 1) * BLOCK, WAVE:]
+                got[w, ka, i * BLOCK : (i + 1) * BLOCK, :] = jnp.concatenate(
+                    [o[:, :WAVE], right], axis=1
+                )
 
     def dense_weigh(g):
         @pl.when(pb == 0)
@@ -221,27 +223,23 @@
 
             def score(b, m):
                 k = kb[pl.ds(b * NKA + base, 4)].reshape(4 * BLOCK, HEAD_DIM)
-                s = nt(q, k) * SCALE
+                s = nt(k, q) * SCALE
                 sg[b] = s
-                for j in range(4):
-                    m = jnp.maximum(m, s[:, j * 128 : (j + 1) * 128])
-                return m
-
-            old = mg[g - 1] if g else jnp.full((DENSE, 128), NEG, F32)
+                return jnp.maximum(m, jnp.max(s, axis=0, keepdims=True))
+
+            old = mg[g - 1, 0:1, :] if g else jnp.full((1, DENSE), NEG, F32)
             m = lax.fori_loop(0, NPB, score, old)
-            m = jnp.broadcast_to(jnp.max(m, axis=1, keepdims=True), (DENSE, 128))
-            mg[g] = m
+            mg[g] = jnp.broadcast_to(m, (8, DENSE))
 
             def expo(b, total):
-                for j in range(4):
-                    p = jnp.exp2(sg[b, :, j * 128 : (j + 1) * 128] - mg[g])
-                    total = total + p
-                    pg[g, b, :, j * 128 : (j + 1) * 128] = p.astype(BF16)
-                return total
-
-            total = lax.fori_loop(0, NPB, expo, jnp.zeros((DENSE, 128), F32))
-            total = jnp.broadcast_to(jnp.sum(total, axis=1, keepdims=True), (DENSE, 128))
-            gtot[...] = total + gtot[...] * jnp.exp2(old - m) if g else total
+                p = jnp.exp2(sg[b] - m)
+                pg[g, b] = p.astype(BF16)
+                return total + jnp.sum(p, axis=0, keepdims=True)
+
+            total = lax.fori_loop(0, NPB, expo, jnp.zeros((1, DENSE), F32))
+            if g:
+                total = total + gtot[0:1, :] * jnp.exp2(old - m)
+            gtot[...] = jnp.broadcast_to(total, (8, DENSE))
 
     def dense_value(w, g):
         @pl.when(pb == 0)
@@ -251,11 +249,10 @@
             def part(b, acc):
                 v = vbs[w][pl.ds(b * NKA + base, 4)]
                 v = jnp.concatenate([v[j] for j in range(4)], axis=1)
-                return acc + nt(pg[g, b], v)
-
-            acc = lax.fori_loop(0, NPB, part, jnp.zeros((DENSE, WAVE), F32))
-            acc = acc * jnp.exp2(mg[g] - mg[3])[:, :WAVE]
-            acc = jnp.concatenate([acc, acc], axis=1)
+                return acc + jnp.dot(v, pg[g, b], preferred_element_type=F32)
+
+            acc = lax.fori_loop(0, NPB, part, jnp.zeros((WAVE, DENSE), F32))
+            acc = acc * jnp.exp2(mg[g, 0:1, :] - mg[3, 0:1, :])
             gacc[w] = gacc[w] + acc if g else acc
 
     def at(dx, dy):
@@ -505,12 +502,12 @@
             vmem((16, 128), jnp.int32),
             pltpu.SMEM((16, 128), jnp.int32),
             vmem((QBLOCKS, SLOTS, BLOCK, BLOCK), BF16),
-            vmem((QBLOCKS, BLOCK, 128), F32),
-            vmem((NPB, DENSE, 4 * BLOCK), F32),
-            vmem((4, NPB, DENSE, 4 * BLOCK), BF16),
-            vmem((4, DENSE, 128), F32),
-            vmem((DENSE, 128), F32),
-            vmem((2, DENSE, 128), F32),
+            vmem((QBLOCKS, 8, 128), F32),
+            vmem((NPB, 4 * BLOCK, DENSE), F32),
+            vmem((4, NPB, 4 * BLOCK, DENSE), BF16),
+            vmem((4, 8, DENSE), F32),
+            vmem((8, DENSE), F32),
+            vmem((2, WAVE, DENSE), F32),
             dma((8,)), dma((12,)), dma((3,)), dma((36,)), dma((2,)), dma((2, 10)),
         ],
         compiler_params=pltpu.CompilerParams(

time: 112 us -> 109 us (0.973)
  Pallas kernels: 107 us -> 104 us
    pallas_call x1, Pallas kernels: 107 us -> 104 us  [attend(): pl.pallas_call(attend_kernel, out_shape=pltpu.VMEM((ROWS, HEADS * HEAD_DI...]
where the time goes in v4:
time: 109 us; the launch traced here: 108 us
  Pallas kernels  104 us (95%)
  local copies, waits for them, and re-layouts  4.68 us (4%)
    pallas_call x1, Pallas kernels, attend(): pl.pallas_call(attend_kernel, out_shape=pltpu.VMEM((ROWS, HEADS * HEAD_DI...  104 us
    unnamed x1, local copies, waits for them, and re-layouts  3.4 us

profile of v4, /device:TPU:0, one launch (start us, length us, event | category | flops | bytes accessed | tf_op | source)
XLA Modules:
  0.0 108.5 jit_solution(12040114967489600485)
XLA Ops:
  0.0 1.3 %pad.4.m_hbm = s32[8,128]{1,0:T(8,128)} pad(s32[8,16]{1,0:T(8,128)} %bitcast.1, s32[]{:T(128)} %constant.0.clone.1), padding=0_0x0_112 | pad | bytes 4612 | tf_op jit(solution)/shard_map/jit(_pad)/pad | solution.py:521
  1.3 103.8 %attend.1 = bf16[2048,2048]{1,0:T(8,128)(2,1)S(1)} custom-call(bf16[2048,2048]{1,0:T(8,128)(2,1)} %q_hbm.1, bf16[128,2048]{1,0:T(8,128)(2,1)} %k_hbm.1, bf16[128,2048]{1,0:T(8,128)(2,1)} %v_hbm.1, s32[8,128]{1,0:T(8,128)} %pad.4.m_hbm), custom_call_target="tpu_custom_call" | custom-call | tf_op jit(solution)/shard_map/attend/pallas_call | solution.py:488
  105.1 3.4 %copy.6 = bf16[2048,2048]{1,0:T(8,128)(2,1)} copy(bf16[2048,2048]{1,0:T(8,128)(2,1)S(1)} %attend.1) | data formatting | bytes 16777216

commit v5 on v4

--- a/solution.py
+++ b/solution.py
@@ -419,28 +419,23 @@
     own(10)
     near(9)
     distant(8)
-    relayed(8)
-    dense_value(1, 0)
     own(11)
-    first.stage(1)
     near(10)
     distant(9)
-    relayed(9)
-    dense_value(1, 1)
+    first.stage(1)
     near(11)
     distant(10)
-    relayed(10)
-    dense_value(1, 2)
     first.stage(2)
     distant(11)
-    relayed(11)
-    dense_value(1, 3)
+    first.stage(3)
+    for g in range(4):
+        relayed(8 + g)
+        dense_value(1, g)
+    first.stage(4)
     value(1)
     second.stage(0)
     for a in both:
         unpack(a, 0, 0, None)
-    first.stage(3)
-    first.stage(4)
     second.stage(1)
     for a in both:
         unpack(a, -1, 0, None)

time: 109 us -> 106 us (0.972)
  Pallas kernels: 104 us -> 101 us
    pallas_call x1, Pallas kernels: 104 us -> 101 us  [attend(): pl.pallas_call(attend_kernel, out_shape=pltpu.VMEM((ROWS, HEADS * HEAD_DI...]
where the time goes in v5:
time: 106 us; the launch traced here: 105 us
  Pallas kernels  101 us (95%)
  local copies, waits for them, and re-layouts  4.68 us (4%)
    pallas_call x1, Pallas kernels, attend(): pl.pallas_call(attend_kernel, out_shape=pltpu.VMEM((ROWS, HEADS * HEAD_DI...  101 us
    unnamed x1, local copies, waits for them, and re-layouts  3.4 us

profile of v5, /device:TPU:0, one launch (start us, length us, event | category | flops | bytes accessed | tf_op | source)
XLA Modules:
  0.0 105.4 jit_solution(9165831905180270709)
XLA Ops:
  0.0 1.3 %pad.4.m_hbm = s32[8,128]{1,0:T(8,128)} pad(s32[8,16]{1,0:T(8,128)} %bitcast.1, s32[]{:T(128)} %constant.0.clone.1), padding=0_0x0_112 | pad | bytes 4612 | tf_op jit(solution)/shard_map/jit(_pad)/pad | solution.py:516
  1.3 100.7 %attend.1 = bf16[2048,2048]{1,0:T(8,128)(2,1)S(1)} custom-call(bf16[2048,2048]{1,0:T(8,128)(2,1)} %q_hbm.1, bf16[128,2048]{1,0:T(8,128)(2,1)} %k_hbm.1, bf16[128,2048]{1,0:T(8,128)(2,1)} %v_hbm.1, s32[8,128]{1,0:T(8,128)} %pad.4.m_hbm), custom_call_target="tpu_custom_call" | custom-call | tf_op jit(solution)/shard_map/attend/pallas_call | solution.py:483
  102.0 3.4 %copy.6 = bf16[2048,2048]{1,0:T(8,128)(2,1)} copy(bf16[2048,2048]{1,0:T(8,128)(2,1)S(1)} %attend.1) | data formatting | bytes 16777216

commit v6 on v5

--- a/solution.py
+++ b/solution.py
@@ -412,11 +412,11 @@
     own(9)
     lax.fori_loop(12, 16, weigh, 0)
     relayed(7)
+    near(8)
+    own(10)
     dense_value(0, 3)
     value(0)
     first.stage(0)
-    near(8)
-    own(10)
     near(9)
     distant(8)
     own(11)

time: 106 us -> 106 us (level)
  no operation moved by 1% of the time
where the time goes in v6:
time: 106 us; the launch traced here: 105 us
  Pallas kernels  101 us (95%)
  local copies, waits for them, and re-layouts  4.68 us (4%)
    pallas_call x1, Pallas kernels, attend(): pl.pallas_call(attend_kernel, out_shape=pltpu.VMEM((ROWS, HEADS * HEAD_DI...  101 us
    unnamed x1, local copies, waits for them, and re-layouts  3.4 us

profile of v6, /device:TPU:0, one launch (start us, length us, event | category | flops | bytes accessed | tf_op | source)
XLA Modules:
  0.0 105.5 jit_solution(7271237258298594609)
XLA Ops:
  0.0 1.3 %pad.4.m_hbm = s32[8,128]{1,0:T(8,128)} pad(s32[8,16]{1,0:T(8,128)} %bitcast.1, s32[]{:T(128)} %constant.0.clone.1), padding=0_0x0_112 | pad | bytes 4612 | tf_op jit(solution)/shard_map/jit(_pad)/pad | solution.py:516
  1.3 100.8 %attend.1 = bf16[2048,2048]{1,0:T(8,128)(2,1)S(1)} custom-call(bf16[2048,2048]{1,0:T(8,128)(2,1)} %q_hbm.1, bf16[128,2048]{1,0:T(8,128)(2,1)} %k_hbm.1, bf16[128,2048]{1,0:T(8,128)(2,1)} %v_hbm.1, s32[8,128]{1,0:T(8,128)} %pad.4.m_hbm), custom_call_target="tpu_custom_call" | custom-call | tf_op jit(solution)/shard_map/attend/pallas_call | solution.py:483
  102.1 3.4 %copy.6 = bf16[2048,2048]{1,0:T(8,128)(2,1)} copy(bf16[2048,2048]{1,0:T(8,128)(2,1)S(1)} %attend.1) | data formatting | bytes 16777216
